TPU v7x, 128 devices: a whole 4x4x4 slice. The times are simulated.
128 devices in a mesh: freq: 8 (over y, core), trace: 16 (over x, z).
Axes of the slice: x: 4, y: 4, z: 4, core: 2. Of those that a mesh axis runs over, the one named last changes fastest.
Arguments:
- traces: bfloat16 [8, 4096, 4096], P('freq', 'trace'), may hold values from -6 to 6
- coords: int32 [4, 8, 4096], replicated, may hold values from 0 to 1023
- wavenumbers: int32 [4, 8, 4096], replicated, may hold values from 0 to 1023
- fold: int32 [8], replicated, may hold values from 512 to 4096, as said below
- selected: int32 [2, 8, 1024], P(None, None, 'freq'), may hold values from 0 to 4095
Outputs:
- spectrum: float32 [4096, 8, 2, 1024], P('trace', None, None, 'freq')
- coefficients: float32 [2, 8, 2, 1024], P(None, None, None, 'freq')
Inputs may be any that keep to these rules, and one draw needn't show every extreme that they name: Slots 0 to fold - 1 of a patch are live, the rest are not; some patch has all 4096 slots live.
All inputs are finite; a program needn't handle non-finite values.
Results may differ from a plain program's by a relative error of at most 0.0052.
Values may be sent and summed in bfloat16 or wider, within the bound.
No kernel may reach another device: no remote copies, remote signals or barrier semaphores. Data moves between devices by JAX's collectives and lax.ppermute only.
A program may use at most 128 MiB of HBM per device.

v0:
```python
import functools
import math

import jax
import jax.numpy as jnp
from jax import lax
from jax.sharding import Mesh
from jax.sharding import PartitionSpec as P

NF = 1024
NK = 4096
GRID = 1024
ITERS = 2
TRACE = ("trace_0", "trace_1")


def one_axis_at_a_time(value, axes):
    return functools.reduce(lax.psum, axes, value)


def dft_table(length, count):
    sample = jnp.arange(length, dtype=jnp.int32)
    bins = jnp.arange(count, dtype=jnp.int32)
    product = sample[:, None] * bins[None, :] % length
    angle = product.astype(jnp.float32) * (2.0 * math.pi / length)
    return jnp.concatenate([jnp.cos(angle), -jnp.sin(angle)], axis=1).astype(jnp.bfloat16)


def partial_spectrum(rows, places, wavenumbers, first_wave, wave_count):
    waves = lax.dynamic_slice_in_dim(wavenumbers, first_wave, wave_count, 2)
    inner = jnp.zeros((rows.shape[0], wave_count, rows.shape[1]), jnp.int32)
    for comp in range(4):
        inner = inner + waves[comp][:, :, None] * places[comp][:, None, :]
    inner = inner % GRID
    angle = inner.astype(jnp.float32) * (2.0 * math.pi / GRID)
    atoms = jnp.concatenate([jnp.cos(angle), jnp.sin(angle)], axis=1).astype(jnp.bfloat16)
    product = jnp.einsum("pks,psf->kpf", atoms, rows, preferred_element_type=jnp.float32)
    half = rows.shape[2] // 2
    s_real = product[:wave_count, :, :half] + product[wave_count:, :, half:]
    s_imag = product[:wave_count, :, half:] - product[wave_count:, :, :half]
    return jnp.stack([s_real, s_imag], axis=2)


def local(traces, coords, wavenumbers, fold, selected):
    slot_count = traces.shape[1]
    length = traces.shape[2]
    table = dft_table(length, NF)
    spectra = jnp.dot(traces.reshape(-1, length), table, preferred_element_type=jnp.float32)
    spectra = spectra.astype(jnp.bfloat16).reshape(traces.shape[0], slot_count, 2, NF)
    moved = lax.all_to_all(spectra, "freq", split_axis=3, concat_axis=0, tiled=True)
    patches = moved.shape[0]
    group_width = moved.shape[3]
    first_slot = lax.axis_index(TRACE) * slot_count
    my_coords = lax.dynamic_slice_in_dim(coords, first_slot, slot_count, 2)
    slot_index = first_slot + jnp.arange(slot_count, dtype=jnp.int32)
    live = (slot_index[None, :] < fold[:, None]).astype(jnp.float32)
    mask = live[:, :, None]
    res_real = moved[:, :, 0, :].astype(jnp.float32) * mask
    res_imag = moved[:, :, 1, :].astype(jnp.float32) * mask
    inverse = 1.0 / fold.astype(jnp.float32)
    gathered = []
    for iteration in range(ITERS):
        chosen = selected[iteration]
        picked = jnp.take_along_axis(
            wavenumbers, jnp.broadcast_to(chosen[None], (4,) + chosen.shape), axis=2
        )
        inner = jnp.zeros((patches, slot_count, group_width), jnp.int32)
        for comp in range(4):
            inner = inner + picked[comp][:, None, :] * my_coords[comp][:, :, None]
        inner = inner % GRID
        angle = inner.astype(jnp.float32) * (2.0 * math.pi / GRID)
        cosine = jnp.cos(angle)
        sine = jnp.sin(angle)
        part_real = jnp.sum(res_real * cosine + res_imag * sine, axis=1)
        part_imag = jnp.sum(res_imag * cosine - res_real * sine, axis=1)
        sum_real, sum_imag = (
            one_axis_at_a_time(part_real, TRACE),
            one_axis_at_a_time(part_imag, TRACE),
        )
        coef_real = sum_real * inverse[:, None]
        coef_imag = sum_imag * inverse[:, None]
        res_real = res_real - mask * (coef_real[:, None, :] * cosine - coef_imag[:, None, :] * sine)
        res_imag = res_imag - mask * (coef_real[:, None, :] * sine + coef_imag[:, None, :] * cosine)
        gathered.append(jnp.stack([coef_real, coef_imag], axis=1))
    rounded = jnp.concatenate([res_real, res_imag], axis=2).astype(jnp.bfloat16)
    wave_share = NK // lax.axis_size(TRACE)
    first_wave = lax.axis_index(TRACE) * wave_share
    spectrum = partial_spectrum(
        lax.all_gather(rounded, TRACE, axis=1, tiled=True),
        coords,
        wavenumbers,
        first_wave,
        wave_share,
    )
    return (spectrum, jnp.stack(gathered, axis=0))


def solution(mesh):
    split = Mesh(mesh.devices.reshape(mesh.shape["freq"], 4, 4), ("freq", "trace_0", "trace_1"))
    return jax.shard_map(
        local,
        mesh=split,
        in_specs=(P("freq", TRACE, None), P(), P(), P(), P(None, None, "freq")),
        out_specs=(P(TRACE, None, None, "freq"), P(None, None, None, "freq")),
        check_vma=False,
    )
```

profile of v0, /device:TPU:0, one launch (start us, length us, event | category | flops | bytes accessed | tf_op | source)
XLA Modules:
  0.0 407.6 jit_solution(8427520909776739140)
XLA Ops:
  7.2 0.0 copy-start
  7.2 68.7 %negate_convert_fusion = (bf16[4096,1024]{1,0:T(8,128)(2,1)}, bf16[4096,1024]{1,0:T(8,128)(2,1)}) fusion(), kind=kLoop, calls=%fused_computation.24 | loop fusion | flops 71303168 | bytes 16777216 | tf_op jit(solution)/shard_map/convert.7
  75.9 0.0 copy-done
  75.9 0.0 copy-start.4
  75.9 0.0 copy-start.5
  75.9 0.0 copy-start.3
  76.0 0.0 copy-start.2
  76.0 8.8 %fusion.17 = bf16[2048,256]{1,0:T(8,128)(2,1)S(1)} fusion(bf16[4096,1024]{1,0:T(8,128)(2,1)} %get-tuple-element.59, bf16[4096,1024]{1,0:T(8,128)(2,1)} %get-tuple-element.60, bf16[1,256,4096]{2,1,0:T(8,128)(2,1)S(1)} %copy-done), kind=kOutput, calls=%fused_computation.29 | convolution fusion | flops 4329046016 | bytes 19922944 | tf_op jit(solution)/shard_map/dot_general | solution.py:48
  84.8 2.0 copy.13
  86.9 4.6 %all-to-all-start = ((bf16[1,256,2,1024]{1,2,0,3:T(2,128)(2,1)}), bf16[1,256,2,1024]{1,2,0,3:T(2,128)(2,1)S(1)}, u32[]{:S(2)}, u32[]{:S(2)}) async-start(bf16[1,256,2,1024]{1,2,0,3:T(2,128)(2,1)} %copy.13), calls=%async_computation | async-start | bytes 2097152 | tf_op jit(solution)/shard_map/all_to_all | solution.py:50
  91.4 0.0 all-gather.2.cloned.1.call-start
  91.5 0.0 copy-done.4
  91.6 0.0 copy-done.5
  91.6 0.1 compare_convert_fusion
  91.7 0.0 copy-done.3
  91.7 0.0 copy-done.2
  91.7 32.0 %gather_fusion = s32[4096]{0:T(1024)S(1)} fusion(s32[4,8,4096]{2,1,0:T(8,128)S(1)} %copy-done.2, s32[4096]{0:T(1024)S(1)} %get-tuple-element.57), kind=kCustom, calls=%fused_computation.clone | custom fusion | bytes 81920 | tf_op jit(solution)/shard_map/jit(take_along_axis)/gather | solution.py:64
  123.7 32.0 %gather_fusion.1 = s32[4096]{0:T(1024)S(1)} fusion(s32[4,8,4096]{2,1,0:T(8,128)S(1)} %copy-done.2, s32[4096]{0:T(1024)S(1)} %get-tuple-element.58), kind=kCustom, calls=%fused_computation.1.clone | custom fusion | bytes 81920 | tf_op jit(solution)/shard_map/jit(take_along_axis)/gather | solution.py:64
  155.7 0.0 all-to-all-done
  155.7 0.1 copy.14
  155.9 6.0 %fusion.36 = (f32[8,128]{1,0:T(8,128)S(1)}, f32[8,128]{1,0:T(8,128)S(1)}) fusion(s32[8,256]{1,0:T(8,128)S(1)} %get-tuple-element.38, s32[8,128]{1,0:T(8,128)S(1)} %get-tuple-element.40, s32[8,256]{1,0:T(8,128)S(1)} %get-tuple-element.36, s32[8,128]{1,0:T(8,128)S(1)} %get-tuple-element.41, s32[8,256]{1,0:T(8,128)S(1)} %get-tuple-element.37, ...), kind=kLoop, calls=%fused_computation.55 | loop fusion | flops 8386560 | bytes 1114112 | tf_op jit(solution)/shard_map/reduce_sum | solution.py:74
  161.9 10.6 %all-reduce.3 = (f32[8,128]{1,0:T(8,128)S(1)}, f32[8,128]{1,0:T(8,128)S(1)}) all-reduce(f32[8,128]{1,0:T(8,128)S(1)} %get-tuple-element.12, f32[8,128]{1,0:T(8,128)S(1)} %get-tuple-element.11), channel_id=1, replica_groups=mesh['freq'=8,'trace_0'=4,'trace_1'=4] {'trace_0'}, use_global_device_ids=true, to_apply=%region_4.6 | all-reduce | flops 2048 | bytes 16384 | tf_op jit(solution)/shard_map/psum | solution.py:18
  172.5 11.9 %all-reduce.1 = (f32[8,128]{1,0:T(8,128)S(1)}, f32[8,128]{1,0:T(8,128)S(1)}) all-reduce(f32[8,128]{1,0:T(8,128)S(1)} %get-tuple-element.19, f32[8,128]{1,0:T(8,128)S(1)} %get-tuple-element.20), channel_id=1, replica_groups=mesh['freq'=8,'trace_0'=4,'trace_1'=4] {'trace_1'}, use_global_device_ids=true, to_apply=%region_5.7 | all-reduce | flops 2048 | bytes 16384 | tf_op jit(solution)/shard_map/psum | solution.py:18
  184.4 0.1 broadcast_multiply_fusion.3
  184.4 11.0 %add_reduce_fusion = (f32[8,128]{1,0:T(8,128)S(1)}, f32[8,128]{1,0:T(8,128)S(1)}) fusion(s32[8,256]{1,0:T(8,128)S(1)} %get-tuple-element.38, s32[8,128]{1,0:T(8,128)S(1)} %get-tuple-element.44, s32[8,256]{1,0:T(8,128)S(1)} %get-tuple-element.36, s32[8,128]{1,0:T(8,128)S(1)} %get-tuple-element.45, s32[8,256]{1,0:T(8,128)S(1)} %get-tuple-element.37, ...), kind=kLoop, calls=%fused_computation.65 | loop fusion | flops 16250880 | bytes 1138688 | tf_op jit(solution)/shard_map/reduce_sum | solution.py:74
  195.5 7.8 %all-reduce.2 = (f32[8,128]{1,0:T(8,128)S(1)}, f32[8,128]{1,0:T(8,128)S(1)}) all-reduce(f32[8,128]{1,0:T(8,128)S(1)} %get-tuple-element.10, f32[8,128]{1,0:T(8,128)S(1)} %get-tuple-element.9), channel_id=1, replica_groups=mesh['freq'=8,'trace_0'=4,'trace_1'=4] {'trace_0'}, use_global_device_ids=true, to_apply=%region_10.12 | all-reduce | flops 2048 | bytes 16384 | tf_op jit(solution)/shard_map/psum | solution.py:18
  203.3 8.0 %all-reduce = (f32[8,128]{1,0:T(8,128)S(1)}, f32[8,128]{1,0:T(8,128)S(1)}) all-reduce(f32[8,128]{1,0:T(8,128)S(1)} %get-tuple-element.17, f32[8,128]{1,0:T(8,128)S(1)} %get-tuple-element.18), channel_id=1, replica_groups=mesh['freq'=8,'trace_0'=4,'trace_1'=4] {'trace_1'}, use_global_device_ids=true, to_apply=%region_11.13 | all-reduce | flops 2048 | bytes 16384 | tf_op jit(solution)/shard_map/psum | solution.py:18
  211.4 0.1 broadcast_multiply_fusion.1
  211.4 16.2 %subtract_convert_fusion.1 = (bf16[8,256,128]{1,2,0:T(8,128)(2,1)S(1)}, bf16[8,256,128]{1,2,0:T(8,128)(2,1)S(1)}) fusion(f32[8,128]{1,0:T(8,128)S(1)} %get-tuple-element.54, f32[8,128]{1,0:T(8,128)S(1)} %get-tuple-element.53, s32[8,256]{1,0:T(8,128)S(1)} %get-tuple-element.38, s32[8,128]{1,0:T(8,128)S(1)} %get-tuple-element.44, ...), kind=kLoop, calls=%fused_computation.63 | loop fusion | flops 17301504 | bytes 2187264 | tf_op jit(solution)/shard_map/convert.4
  227.6 1.0 pad_maximum_fusion.1
  228.7 0.0 all-gather.2.cloned.1.call-update
  228.8 142.7 %cosine_convert_fusion = (bf16[8,256,4096]{2,1,0:T(8,128)(2,1)}, bf16[8,256,4096]{2,1,0:T(8,128)(2,1)}) fusion(s32[8,4096]{1,0:T(8,128)S(1)} %get-tuple-element.33, s32[8,256]{1,0:T(8,128)S(1)} %get-tuple-element.30, s32[8,4096]{1,0:T(8,128)S(1)} %get-tuple-element.34, s32[8,256]{1,0:T(8,128)S(1)} %get-tuple-element.28, s32[8,4096]{1,0:T(8,128)S(1)} %get-tuple-element.32, ...), kind=kLoop, calls=%fused_computation.13 | loop fusion | flops 184549376 | bytes 34111488 | tf_op jit(solution)/shard_map/convert.2
  371.5 0.6 pad_maximum_fusion.2
  372.1 0.0 all-gather.2.cloned.1.call-done
  372.1 0.0 copy-start.1
  372.1 20.4 %fusion.20 = f32[512,8,256]{0,2,1:T(8,128)} fusion(bf16[8,4096,256]{1,2,0:T(8,128)(2,1)} %all-gather.2.cloned.1.call-done, bf16[8,256,4096]{2,1,0:T(8,128)(2,1)} %get-tuple-element.26, bf16[8,256,4096]{2,1,0:T(8,128)(2,1)} %get-tuple-element.25), kind=kOutput, calls=%fused_computation.30 | convolution fusion | flops 8657043456 | bytes 54525952 | tf_op jit(solution)/shard_map/pks,psf->kpf/dot_general | solution.py:37
  392.5 2.5 fusion.31
  395.1 1.6 pad_maximum_fusion
  396.6 4.1 %copy.17 = f32[256,8,2,128]{3,2,1,0:T(2,128)} copy(f32[256,8,2,128]{0,3,1,2:T(8,128)} %pad_maximum_fusion) | data formatting | bytes 4194304
  400.8 0.0 copy-done.1
  (16 shorter events, 0.2 us)
Async XLA Ops:
  7.2 68.8 %copy-start = (bf16[1,256,4096]{2,1,0:T(8,128)(2,1)S(1)}, bf16[1,256,4096]{2,1,0:T(8,128)(2,1)}, u32[]{:S(2)}) copy-start(bf16[1,256,4096]{2,1,0:T(8,128)(2,1)} %param.7) | copy-start | bytes 6291460
  75.9 15.6 %copy-start.4 = (s32[2,8,128]{2,1,0:T(8,128)S(1)}, s32[2,8,128]{2,1,0:T(8,128)}, u32[]{:S(2)}) copy-start(s32[2,8,128]{2,1,0:T(8,128)} %param.11) | copy-start | bytes 24580
  75.9 15.6 %copy-start.5 = (s32[8]{0:T(128)S(1)}, s32[8]{0:T(128)}, u32[]{:S(2)}) copy-start(s32[8]{0:T(128)} %param.10) | copy-start | bytes 100
  75.9 15.7 %copy-start.3 = (s32[4,8,4096]{2,1,0:T(8,128)S(1)}, s32[4,8,4096]{2,1,0:T(8,128)}, u32[]{:S(2)}) copy-start(s32[4,8,4096]{2,1,0:T(8,128)} %param.8) | copy-start | bytes 1572868
  76.0 15.8 %copy-start.2 = (s32[4,8,4096]{2,1,0:T(8,128)S(1)}, s32[4,8,4096]{2,1,0:T(8,128)}, u32[]{:S(2)}) copy-start(s32[4,8,4096]{2,1,0:T(8,128)} %param.9) | copy-start | bytes 1572868
  86.9 68.9 %all-to-all-start = ((bf16[1,256,2,1024]{1,2,0,3:T(2,128)(2,1)}), bf16[1,256,2,1024]{1,2,0,3:T(2,128)(2,1)S(1)}, u32[]{:S(2)}, u32[]{:S(2)}) async-start(bf16[1,256,2,1024]{1,2,0,3:T(2,128)(2,1)} %copy.13), calls=%async_computation | async-start | bytes 2097152 | tf_op jit(solution)/shard_map/all_to_all | solution.py:50
  91.4 280.6 %all-gather.2.cloned.1.call-start = ((), (), s32[]{:S(2)}) async-start(), calls=%async_computation.1 | async-start | bytes 17825792 | tf_op jit(solution)/shard_map/all_gather | solution.py:89
  372.1 28.7 %copy-start.1 = (bf16[1,256,4096]{2,1,0:T(8,128)(2,1)S(1)}, bf16[1,256,4096]{2,1,0:T(8,128)(2,1)}, u32[]{:S(2)}) copy-start(bf16[1,256,4096]{2,1,0:T(8,128)(2,1)} %param.7) | copy-start | bytes 6291460
Sparse Core Ops, SparseCore 0:
  228.8 119.5 all-gather.1
where the time goes:
time: 409 us; the launch traced here: 408 us
  other arithmetic  251 us (61%)
  local copies, waits for them, and re-layouts  70.4 us (17%)
  blocking collectives  38.4 us (9%)
  matrix products  29.3 us (7%)
  between operations  14.3 us (3%)
  starting transfers between devices  4.62 us (1%)
    another operation x3, other arithmetic  228 us
    gather x2, local copies, waits for them, and re-layouts, local(): jnp.take_along_axis(wavenumbers, jnp.broadcast_to(chosen[None], (4,) + ch...  64 us
    psum x4, blocking collectives, one_axis_at_a_time(): return functools.reduce(lax.psum, axes, value)  38.4 us
    dot_general x1, matrix products, partial_spectrum(): jnp.einsum('pks,psf->kpf', atoms, rows, preferred_element_type=jnp.float32)  20.4 us
    reduce_sum x2, other arithmetic, local(): part_real = jnp.sum(res_real * cosine + res_imag * sine, axis=1)  17 us
    dot_general x1, matrix products, local(): jnp.dot(traces.reshape(-1, length), table, preferred_element_type=jnp.flo...  8.84 us
  transfers between devices with their start and end apart: 2, of which 0 were waited for; matrix products, arithmetic and copies ran while one was open for 51% of the time, Pallas kernels for 0%

commit v1 on v0

v1 whole, which is shorter than its diff:
```python
import math

import jax
import jax.numpy as jnp
from jax import lax
from jax.experimental import pallas as pl
from jax.experimental.pallas import tpu as pltpu
from jax.sharding import Mesh
from jax.sharding import PartitionSpec as P

BF = jnp.bfloat16
F32 = jnp.float32
NT = 4096
SLOTS = 4096
GRID = 1024
TRACE = ("half", "xl", "z")
EIGHT = ("xl", "z")
ROUND = 12582912.0
R2 = math.sqrt(2.0)
VMEM = 58 << 20


def dot(a, b):
    return jnp.dot(a, b, preferred_element_type=F32)


def to_turn(t):
    return t - ((t + ROUND) - ROUND)


def cos_sin(r):
    y = r * r
    s = r * (
        R2 * 3.14159258
        + y * (R2 * -5.16770688 + y * (R2 * 2.55003138 + y * (R2 * -0.59804517 + y * (R2 * 0.07722012))))
    )
    c = R2 * 0.99999995 + y * (
        R2 * -4.93479286 + y * (R2 * 4.05841192 + y * (R2 * -1.33188016 + y * (R2 * 0.2196968)))
    )
    return 1.0 - s * s, s * c


def cos_sin_short(r):
    y = r * r
    s = r * (R2 * 3.14158202 + y * (R2 * -5.16714279 + y * (R2 * 2.541899 + y * (R2 * -0.55463613))))
    c = R2 * 0.9999933 + y * (R2 * -4.93393802 + y * (R2 * 4.04128385 + y * (R2 * -1.22212706)))
    return 1.0 - s * s, s * c


def low_high(v):
    high = v >> 5
    return (v & 31).astype(F32), high.astype(F32)


def wave_rows(w):
    low, high = low_high(w)
    return jnp.concatenate([high * (1 / 32), low * (1 / 32), low * (1 / 1024), jnp.zeros_like(low)], axis=0)


def place_rows(x):
    low, high = low_high(x)
    return jnp.concatenate([low, high, low, jnp.zeros_like(low)], axis=0)


def dft(traces, part):
    def body(x_ref, o_ref):
        f = pl.program_id(0) * 256 + lax.broadcasted_iota(jnp.int32, (64, 256), 1)
        n = lax.broadcasted_iota(jnp.int32, (64, 256), 0)

        def table(step):
            m = (n * f * step) & (NT - 1)
            m = jnp.where(m >= NT // 2, m - NT, m)
            return cos_sin(m.astype(F32) * (1.0 / NT))

        c_far, s_far = table(64)
        c_near, s_near = table(1)
        acc = jnp.zeros((256, 256), F32)
        for chunk in range(NT // 256):
            rows = []
            for a in range(chunk * 4, chunk * 4 + 4):
                ca, sa = c_far[a : a + 1, :], s_far[a : a + 1, :]
                if part == 0:
                    rows.append(ca * c_near - sa * s_near)
                else:
                    rows.append(-(sa * c_near) - ca * s_near)
            acc = acc + dot(x_ref[:, chunk * 256 : (chunk + 1) * 256], jnp.concatenate(rows, axis=0).astype(BF))
        o_ref[0] = acc[:, :128].astype(BF)
        o_ref[1] = acc[:, 128:].astype(BF)

    return pl.pallas_call(
        body,
        grid=(4,),
        out_shape=jax.ShapeDtypeStruct((8, 256, 128), BF),
        in_specs=[pl.BlockSpec((256, NT), lambda i: (0, 0))],
        out_specs=pl.BlockSpec((2, 256, 128), lambda i: (i, 0, 0)),
        compiler_params=pltpu.CompilerParams(vmem_limit_bytes=VMEM),
        cost_estimate=pl.CostEstimate(flops=2 * 256 * NT * 1024, bytes_accessed=3 << 20, transcendentals=0),
        name="dft" + str(part),
    )(traces)


def make_atoms(waves, places):
    rows = 256

    def body(w_ref, x_ref, o_ref):
        w = jnp.transpose(wave_rows(w_ref[...])).astype(BF)
        x = place_rows(x_ref[...]).astype(BF)
        for j in range(16):
            c, s = cos_sin_short(to_turn(dot(w, x[:, j * 256 : (j + 1) * 256])))
            o_ref[:, j * 256 : (j + 1) * 256] = c.astype(BF)
            o_ref[:, SLOTS + j * 256 : SLOTS + (j + 1) * 256] = s.astype(BF)

    count = waves.shape[1]
    return pl.pallas_call(
        body,
        grid=(count // rows,),
        out_shape=jax.ShapeDtypeStruct((count, 2 * SLOTS), BF),
        in_specs=[pl.BlockSpec((4, rows), lambda i: (0, i)), pl.BlockSpec((4, SLOTS), lambda i: (0, 0))],
        out_specs=pl.BlockSpec((rows, 2 * SLOTS), lambda i: (i, 0)),
        compiler_params=pltpu.CompilerParams(vmem_limit_bytes=VMEM),
        cost_estimate=pl.CostEstimate(flops=30 << 30, bytes_accessed=count * 16384, transcendentals=0),
        name="atoms",
    )(waves, places)


def pursue(real, imag, places, waves, chosen, fold):
    blocks, size = 16, 256

    def body(fold_ref, re_ref, im_ref, x_ref, w_ref, ch_ref, o_ref, co_ref, ec_ref, es_ref):
        table3 = w_ref[0] + w_ref[1] * 1024 + w_ref[2] * (1 << 20)
        index = jnp.concatenate([ch_ref[...]] * 4, axis=0)
        low, high = index & 127, index >> 7
        found3 = jnp.zeros((8, 128), jnp.int32)
        found1 = jnp.zeros((8, 128), jnp.int32)
        for r in range(32):
            here = high == r
            g3 = jnp.take_along_axis(jnp.broadcast_to(table3[r : r + 1], (8, 128)), low, axis=1)
            g1 = jnp.take_along_axis(jnp.broadcast_to(w_ref[3, r : r + 1], (8, 128)), low, axis=1)
            found3 = jnp.where(here, g3, found3)
            found1 = jnp.where(here, g1, found1)
        parts = [found3 & 1023, (found3 >> 10) & 1023, found3 >> 20, found1]
        picked = jnp.concatenate(
            [jnp.concatenate([v[t : t + 1] for v in parts], axis=0) for t in range(2)], axis=1
        )
        w = wave_rows(picked).astype(BF)
        count = fold_ref[0]
        inverse = 1.0 / count.astype(F32)
        zero = jnp.zeros((8, 128), F32)

        def fold8(v):
            return jnp.sum(v.reshape(size // 8, 8, 128), axis=0)

        def gather(j, sums):
            start = pl.multiple_of(j * size, size)
            rows = pl.ds(start, size)
            x = jnp.transpose(place_rows(x_ref[:, rows])).astype(BF)
            c, s = cos_sin(to_turn(dot(x, w)))
            ec_ref[rows, :] = c
            es_ref[rows, :] = s
            live = (start + lax.broadcasted_iota(jnp.int32, (size, 128), 0)) < count
            re = jnp.where(live, re_ref[rows, :].astype(F32), 0.0)
            im = jnp.where(live, im_ref[rows, :].astype(F32), 0.0)
            c0, c1, s0, s1 = c[:, :128], c[:, 128:], s[:, :128], s[:, 128:]
            new = (
                re * c0 + im * s0,
                im * c0 - re * s0,
                re * c1 + im * s1,
                im * c1 - re * s1,
                jnp.where(live, c0 * c1 + s0 * s1, 0.0),
                jnp.where(live, s0 * c1 - c0 * s1, 0.0),
            )
            return tuple(a + fold8(b) for a, b in zip(sums, new))

        sums = lax.fori_loop(0, blocks, gather, (zero,) * 6)
        r0, i0, r1, i1, gr, gi = [jnp.sum(v, axis=0, keepdims=True) for v in sums]
        a0, b0 = r0 * inverse, i0 * inverse
        a1 = (r1 - (a0 * gr - b0 * gi)) * inverse
        b1 = (i1 - (a0 * gi + b0 * gr)) * inverse

        def split(v):
            first = v.astype(BF).astype(F32)
            second = (v - first).astype(BF).astype(F32)
            return [first, second, v - first - second]

        packed = [jnp.concatenate(pair, axis=1) for pair in zip(split(a0), split(b0))]
        packed += [jnp.concatenate(pair, axis=1) for pair in zip(split(a1), split(b1))]
        co_ref[...] = jnp.concatenate(packed + [jnp.zeros((10, 256), F32)], axis=0).astype(BF)

        def subtract(j, carry):
            start = pl.multiple_of(j * size, size)
            rows = pl.ds(start, size)
            c, s = ec_ref[rows, :], es_ref[rows, :]
            live = (start + lax.broadcasted_iota(jnp.int32, (size, 128), 0)) < count
            c0, c1, s0, s1 = c[:, :128], c[:, 128:], s[:, :128], s[:, 128:]
            re = re_ref[rows, :].astype(F32) - (a0 * c0 - b0 * s0) - (a1 * c1 - b1 * s1)
            im = im_ref[rows, :].astype(F32) - (a0 * s0 + b0 * c0) - (a1 * s1 + b1 * c1)
            re = jnp.where(live, re, 0.0)
            im = jnp.where(live, im, 0.0)
            o_ref[0, rows, :128] = re.astype(BF)
            o_ref[0, rows, 128:] = im.astype(BF)
            o_ref[1, rows, :128] = im.astype(BF)
            o_ref[1, rows, 128:] = (-re).astype(BF)
            return carry

        lax.fori_loop(0, blocks, subtract, 0)

    whole = pl.BlockSpec(memory_space=pltpu.VMEM)
    return pl.pallas_call(
        body,
        out_shape=(jax.ShapeDtypeStruct((2, SLOTS, 256), BF), jax.ShapeDtypeStruct((16, 256), BF)),
        in_specs=[pl.BlockSpec(memory_space=pltpu.SMEM)] + [whole] * 5,
        out_specs=(whole, whole),
        scratch_shapes=[pltpu.VMEM((SLOTS, 256), F32), pltpu.VMEM((SLOTS, 256), F32)],
        compiler_params=pltpu.CompilerParams(vmem_limit_bytes=VMEM),
        cost_estimate=pl.CostEstimate(flops=6 << 30, bytes_accessed=6 << 20, transcendentals=0),
        name="pursue",
    )(fold, real, imag, places, waves, chosen)


def project(atoms, residual, extra, first):
    tall = 144 if extra is not None else 128

    def body(a_ref, r_ref, *rest):
        o_ref = rest[-1]
        acc = dot(a_ref[:, :SLOTS], r_ref[0]) + dot(a_ref[:, SLOTS:], r_ref[1])
        for b in range(4):
            o_ref[b, :128, :] = acc[b * 128 : (b + 1) * 128].astype(BF)
            if extra is not None:
                o_ref[b, 128:, :] = rest[0][...]

    more = [] if extra is None else [extra]
    return pl.pallas_call(
        body,
        grid=(2,),
        out_shape=jax.ShapeDtypeStruct((8, tall, 256), BF),
        in_specs=[
            pl.BlockSpec((512, 2 * SLOTS), lambda i: (i + first, 0)),
            pl.BlockSpec((2, SLOTS, 256), lambda i: (0, 0, 0)),
        ]
        + [pl.BlockSpec((16, 256), lambda i: (0, 0))] * len(more),
        out_specs=pl.BlockSpec((4, tall, 256), lambda i: (i, 0, 0)),
        compiler_params=pltpu.CompilerParams(vmem_limit_bytes=VMEM),
        cost_estimate=pl.CostEstimate(flops=2 * 1024 * 8192 * 256, bytes_accessed=22 << 20, transcendentals=0),
        name="project" + str(first),
    )(atoms, residual, *more)


def finish(first, second):
    step = 32

    def body(a_ref, b_ref, e_ref, o_ref, c_ref):
        for p in range(8):
            for part in range(2):
                lanes = pl.ds(part * 128, 128)
                spread = pl.ds(2 * p + part, step, stride=16)
                o_ref[0, spread, :] = a_ref[p, :, lanes].astype(F32)
                o_ref[1, spread, :] = b_ref[p, :, lanes].astype(F32)

        @pl.when(pl.program_id(0) == 0)
        def _():
            for p in range(8):
                v = e_ref[p].astype(F32)
                for t in range(2):
                    total = v[3 * t : 3 * t + 1] + (v[3 * t + 1 : 3 * t + 2] + v[3 * t + 2 : 3 * t + 3])
                    row = t * 16 + 2 * p
                    c_ref[row : row + 1, :] = total[:, :128]
                    c_ref[row + 1 : row + 2, :] = total[:, 128:]

    return pl.pallas_call(
        body,
        grid=(128 // step,),
        out_shape=(jax.ShapeDtypeStruct((2, 2048, 128), F32), jax.ShapeDtypeStruct((32, 128), F32)),
        in_specs=[
            pl.BlockSpec((8, step, 256), lambda i: (0, i, 0)),
            pl.BlockSpec((8, step, 256), lambda i: (0, i, 0)),
            pl.BlockSpec((8, 16, 256), lambda i: (0, 8, 0)),
        ],
        out_specs=(
            pl.BlockSpec((2, step * 16, 128), lambda i: (0, i, 0)),
            pl.BlockSpec((32, 128), lambda i: (0, 0)),
        ),
        compiler_params=pltpu.CompilerParams(vmem_limit_bytes=VMEM),
        cost_estimate=pl.CostEstimate(flops=1 << 20, bytes_accessed=3 << 20, transcendentals=0),
        name="finish",
    )(first, second, first)


def local(traces, coords, wavenumbers, fold, selected):
    patch = lax.axis_index(EIGHT)
    half = lax.axis_index("half")
    places = lax.dynamic_slice_in_dim(coords, patch, 1, 1)[:, 0]
    waves = lax.dynamic_slice_in_dim(wavenumbers, patch, 1, 1)[:, 0]
    chosen = lax.dynamic_slice_in_dim(selected, patch, 1, 1)[:, 0]
    count = lax.dynamic_slice_in_dim(fold, patch, 1, 0)
    mine = lax.dynamic_slice_in_dim(waves, half * 2048, 2048, 1)
    mine = mine.reshape(4, 8, 2, 128).transpose(0, 2, 1, 3).reshape(4, 2048)

    received = []
    for part in range(2):
        sent = dft(traces[0], part)
        moved = lax.all_to_all(sent, "freq", split_axis=0, concat_axis=0, tiled=True)
        both = jnp.concatenate([moved, moved], axis=0)
        moved = lax.all_to_all(both, TRACE, split_axis=0, concat_axis=0, tiled=True)
        received.append(moved.reshape(SLOTS, 128))
    atoms = make_atoms(mine, places)
    residual, coefs = pursue(received[0], received[1], places, waves.reshape(4, 32, 128), chosen, count)
    first = lax.all_to_all(project(atoms, residual, coefs, 0), EIGHT, split_axis=0, concat_axis=0, tiled=True)
    second = lax.all_to_all(project(atoms, residual, None, 2), EIGHT, split_axis=0, concat_axis=0, tiled=True)
    spectrum, coefficients = finish(first, second)
    return spectrum.reshape(256, 8, 2, 128), coefficients.reshape(2, 8, 2, 128)


def solution(mesh):
    split = Mesh(mesh.devices.reshape(8, 2, 2, 4), ("freq",) + TRACE)
    return jax.shard_map(
        local,
        mesh=split,
        in_specs=(P("freq", TRACE, None), P(), P(), P(), P(None, None, "freq")),
        out_specs=(P(TRACE, None, None, "freq"), P(None, None, None, "freq")),
        check_vma=False,
    )
```

time: 409 us -> 156 us (0.38)
  other arithmetic: 251 us -> 2.14 us
  Pallas kernels: 0 us -> 80.6 us
  local copies, waits for them, and re-layouts: 70.4 us -> 6.52 us
  matrix products: 29.3 us -> 0 us
  waiting for transfers between devices: 0.02 us -> 25.3 us
  blocking collectives: 38.4 us -> 15 us
  starting transfers between devices: 4.62 us -> 25.1 us
  between operations: 14.3 us -> 0.71 us
    another operation x8 -> x0, other arithmetic: 232 us -> none
    pallas_call x0 -> x7, Pallas kernels: none -> 80.6 us  [the longest x1 28.8 us: make_atoms(): pl.pallas_call(body, grid=(count // rows,), out_shape=jax.ShapeDtypeStruc...]
    gather x2 -> x0, local copies, waits for them, and re-layouts: 64 us -> none  [local(): jnp.take_along_axis(wavenumbers, jnp.broadcast_to(chosen[None], (4,) + ch...]
    psum x4 -> x0, blocking collectives: 38.4 us -> none  [one_axis_at_a_time(): return functools.reduce(lax.psum, axes, value)]
    dot_general x2 -> x0, matrix products: 29.3 us -> none  [the longest x1 20.4 us: partial_spectrum(): jnp.einsum('pks,psf->kpf', atoms, rows, preferred_element_type=jnp.float32)]
    all_to_all x1 -> x5, waiting for transfers between devices: 0.01 us -> 25.3 us  [the longest x2 13.4 us: local(): lax.all_to_all(sent, 'freq', split_axis=0, concat_axis=0, tiled=True)]
    all_to_all x1 -> x5, starting transfers between devices: 4.58 us -> 25.1 us  [the longest x2 11.5 us: local(): moved = lax.all_to_all(both, TRACE, split_axis=0, concat_axis=0, tiled=True)]
    reduce_sum x2 -> x0, other arithmetic: 17 us -> none  [local(): part_real = jnp.sum(res_real * cosine + res_imag * sine, axis=1)]
  transfers between devices with their start and end apart: 2 -> 5, of which waited for: 0 -> 3; matrix products, arithmetic and copies ran while one was open for 51% -> 5% of each run, Pallas kernels for 0% -> 29%
where the time goes in v1:
time: 156 us; the launch traced here: 155 us
  Pallas kernels  80.6 us (52%)
  waiting for transfers between devices  25.3 us (16%)
  starting transfers between devices  25.1 us (16%)
  blocking collectives  15 us (10%)
  local copies, waits for them, and re-layouts  6.52 us (4%)
  other arithmetic  2.14 us (1%)
    pallas_call x1, Pallas kernels, make_atoms(): pl.pallas_call(body, grid=(count // rows,), out_shape=jax.ShapeDtypeStruc...  28.8 us
    pallas_call x2, Pallas kernels, project(): pl.pallas_call(body, grid=(2,), out_shape=jax.ShapeDtypeStruct((8, tall,...  20 us
    pallas_call x1, Pallas kernels, pursue(): pl.pallas_call(body, out_shape=(jax.ShapeDtypeStruct((2, SLOTS, 256), BF)...  15 us
    all_to_all x1, blocking collectives, local(): lax.all_to_all(project(atoms, residual, coefs, 0), EIGHT, split_axis=0, c...  15 us
    all_to_all x2, waiting for transfers between devices, local(): lax.all_to_all(sent, 'freq', split_axis=0, concat_axis=0, tiled=True)  13.4 us
    pallas_call x2, Pallas kernels, dft(): pl.pallas_call(body, grid=(4,), out_shape=jax.ShapeDtypeStruct((8, 256, 1...  12.7 us
    all_to_all x2, waiting for transfers between devices, local(): moved = lax.all_to_all(both, TRACE, split_axis=0, concat_axis=0, tiled=True)  11.9 us
    all_to_all x2, starting transfers between devices, local(): moved = lax.all_to_all(both, TRACE, split_axis=0, concat_axis=0, tiled=True)  11.5 us
  transfers between devices with their start and end apart: 5, of which 3 were waited for; matrix products, arithmetic and copies ran while one was open for 5% of the time, Pallas kernels for 29%

profile of v1, /device:TPU:0, one launch (start us, length us, event | category | flops | bytes accessed | tf_op | source)
XLA Modules:
  0.0 155.4 jit_solution(3631813007036823919)
XLA Ops:
  0.6 0.0 copy-start
  0.6 6.6 %dft1.1 = bf16[8,256,128]{2,1,0:T(8,128)(2,1)} custom-call(bf16[256,4096]{1,0:T(8,128)(2,1)} %bitcast.29), custom_call_target="tpu_custom_call" | custom-call | flops 2147483648 | bytes 3145728 | tf_op jit(solution)/shard_map/dft1/pallas_call | solution.py:90
  7.2 4.6 %all-to-all-start.2 = ((bf16[8,256,128]{2,1,0:T(8,128)(2,1)}), bf16[8,256,128]{2,1,0:T(8,128)(2,1)S(1)}, u32[]{:S(2)}, u32[]{:S(2)}) async-start(bf16[8,256,128]{2,1,0:T(8,128)(2,1)} %dft1.1), calls=%async_computation.2 | async-start | bytes 1048576 | tf_op jit(solution)/shard_map/all_to_all | solution.py:301
  11.8 6.1 %dft0.1 = bf16[8,256,128]{2,1,0:T(8,128)(2,1)} custom-call(bf16[256,4096]{1,0:T(8,128)(2,1)} %bitcast.30), custom_call_target="tpu_custom_call" | custom-call | flops 2147483648 | bytes 3145728 | tf_op jit(solution)/shard_map/dft0/pallas_call | solution.py:90
  17.9 4.2 %all-to-all-done.2 = bf16[8,256,128]{2,1,0:T(8,128)(2,1)S(1)} async-done(((bf16[8,256,128]{2,1,0:T(8,128)(2,1)}), bf16[8,256,128]{2,1,0:T(8,128)(2,1)S(1)}, u32[]{:S(2)}, u32[]{:S(2)}) %all-to-all-start.2) | async-done | bytes 524320 | tf_op jit(solution)/shard_map/all_to_all | solution.py:301
  22.1 3.5 %all-to-all-start = ((bf16[8,256,128]{2,1,0:T(8,128)(2,1)}), bf16[8,256,128]{2,1,0:T(8,128)(2,1)S(1)}, u32[]{:S(2)}, u32[]{:S(2)}) async-start(bf16[8,256,128]{2,1,0:T(8,128)(2,1)} %dft0.1), calls=%async_computation | async-start | bytes 1048576 | tf_op jit(solution)/shard_map/all_to_all | solution.py:301
  25.6 1.1 pad_maximum_fusion.1
  26.7 9.2 %all-to-all-done = bf16[8,256,128]{2,1,0:T(8,128)(2,1)S(1)} async-done(((bf16[8,256,128]{2,1,0:T(8,128)(2,1)}), bf16[8,256,128]{2,1,0:T(8,128)(2,1)S(1)}, u32[]{:S(2)}, u32[]{:S(2)}) %all-to-all-start) | async-done | bytes 524320 | tf_op jit(solution)/shard_map/all_to_all | solution.py:301
  35.8 7.9 %all-to-all-start.3 = ((bf16[16,256,128]{2,1,0:T(8,128)(2,1)}), bf16[16,256,128]{2,1,0:T(8,128)(2,1)S(1)}, u32[]{:S(2)}, u32[]{:S(2)}) async-start(bf16[16,256,128]{2,1,0:T(8,128)(2,1)} %pad_maximum_fusion.1), calls=%async_computation.3 | async-start | bytes 2097152 | tf_op jit(solution)/shard_map/all_to_all | solution.py:303
  43.7 1.1 constant_dynamic-slice_fusion.3
  44.9 0.6 copy.14
  45.5 1.9 %constant_dynamic-slice_fusion.1 = (s32[4,1,4096]{2,1,0:T(1,128)}, s32[4,1,4096]{2,1,0:T(1,128)S(1)}) fusion(s32[4,8,4096]{2,1,0:T(8,128)} %param.7, s32[]{:T(128)S(6)} %select_n.13, s32[4,8,4096]{2,1,0:T(8,128)} %param.6), kind=kLoop, calls=%fused_computation.6 | loop fusion | bytes 262148 | tf_op jit(solution)/shard_map/dynamic_slice | solution.py:292
  47.4 0.7 copy.13
  48.0 1.1 pad_maximum_fusion
  49.1 11.9 %all-to-all-done.3 = bf16[16,256,128]{2,1,0:T(8,128)(2,1)S(1)} async-done(((bf16[16,256,128]{2,1,0:T(8,128)(2,1)}), bf16[16,256,128]{2,1,0:T(8,128)(2,1)S(1)}, u32[]{:S(2)}, u32[]{:S(2)}) %all-to-all-start.3) | async-done | bytes 1048608 | tf_op jit(solution)/shard_map/all_to_all | solution.py:303
  61.1 0.0 copy-start.2
  61.1 3.7 %all-to-all-start.1 = ((bf16[16,256,128]{2,1,0:T(8,128)(2,1)}), bf16[16,256,128]{2,1,0:T(8,128)(2,1)S(1)}, u32[]{:S(2)}, u32[]{:S(2)}) async-start(bf16[16,256,128]{2,1,0:T(8,128)(2,1)} %pad_maximum_fusion), calls=%async_computation.1 | async-start | bytes 2097152 | tf_op jit(solution)/shard_map/all_to_all | solution.py:303
  64.7 0.0 copy-start.4
  64.7 28.8 %atoms.1.a_ref = bf16[2048,8192]{1,0:T(8,128)(2,1)} custom-call(s32[4,2048]{1,0:T(4,128)} %bitcast.27, s32[4,4096]{1,0:T(4,128)} %bitcast.24), custom_call_target="tpu_custom_call" | custom-call | flops 32212254720 | bytes 33554432 | tf_op jit(solution)/shard_map/atoms/pallas_call | solution.py:114
  93.6 0.0 copy-done.2
  93.6 0.0 copy-done.4
  93.6 0.6 dynamic_slice.17.fold_ref
  94.2 0.0 copy-done
  94.2 0.6 constant_dynamic-slice_fusion
  94.8 0.0 all-to-all-done.1
  94.8 0.0 copy-start.3
  94.8 1.0 copy-done.3
  95.8 15.0 %pursue.1 = (bf16[2,4096,256]{2,1,0:T(8,128)(2,1)}, bf16[16,256]{1,0:T(8,128)(2,1)}) custom-call(s32[1]{0:T(128)} %dynamic_slice.17.fold_ref, bf16[4096,128]{1,0:T(8,128)(2,1)} %bitcast.21, bf16[4096,128]{1,0:T(8,128)(2,1)} %bitcast.20, s32[4,4096]{1,0:T(4,128)} %bitcast.25, s32[4,32,128]{2,1,0:T(8,128)} %bitcast.26, s32[2,128]{1,0:T(2,128)} %bitcast.28), custom_call_target="tpu_custom_call" | custom-call | flops 6442450944 | bytes 6291456 | tf_op jit(solution)/shard_map/pursue/pallas_call | solution.py:208
  110.8 10.0 %project2.1 = bf16[8,128,256]{2,1,0:T(8,128)(2,1)} custom-call(bf16[2048,8192]{1,0:T(8,128)(2,1)} %atoms.1.a_ref, bf16[2,4096,256]{2,1,0:T(8,128)(2,1)} %get-tuple-element.6.r_ref), custom_call_target="tpu_custom_call" | custom-call | flops 4294967296 | bytes 23068672 | tf_op jit(solution)/shard_map/project2/pallas_call | solution.py:232
  120.8 5.5 %all-to-all-start.5 = ((bf16[8,128,256]{2,1,0:T(8,128)(2,1)}), bf16[8,128,256]{2,1,0:T(8,128)(2,1)S(1)}, u32[]{:S(2)}, u32[]{:S(2)}) async-start(bf16[8,128,256]{2,1,0:T(8,128)(2,1)} %project2.1), calls=%async_computation.5 | async-start | bytes 1048576 | tf_op jit(solution)/shard_map/all_to_all | solution.py:308
  126.3 10.0 %project0.1 = bf16[8,144,256]{2,1,0:T(8,128)(2,1)} custom-call(bf16[2048,8192]{1,0:T(8,128)(2,1)} %atoms.1.a_ref, bf16[2,4096,256]{2,1,0:T(8,128)(2,1)} %get-tuple-element.6.r_ref, bf16[16,256]{1,0:T(8,128)(2,1)} %get-tuple-element.7.rest_0_), custom_call_target="tpu_custom_call" | custom-call | flops 4294967296 | bytes 23068672 | tf_op jit(solution)/shard_map/project0/pallas_call | solution.py:232
  136.4 0.0 all-to-all-done.5.b_ref
  136.4 0.0 copy-start.1
  136.4 15.0 %all_to_all.30.a_ref.e_ref = bf16[8,144,256]{2,1,0:T(8,128)(2,1)} all-to-all(bf16[8,144,256]{2,1,0:T(8,128)(2,1)} %project0.1), channel_id=1, replica_groups=mesh['freq'=8,'half'=2,'xl'=2,'z'=4] {'xl','z'}, dimensions={0} | all-to-all | bytes 1179648 | tf_op jit(solution)/shard_map/all_to_all | solution.py:307
  151.3 0.0 copy-done.1
  151.3 4.1 %finish.1 = (f32[2,2048,128]{2,1,0:T(8,128)}, f32[32,128]{1,0:T(8,128)}) custom-call(bf16[8,144,256]{2,1,0:T(8,128)(2,1)} %all_to_all.30.a_ref.e_ref, bf16[8,128,256]{2,1,0:T(8,128)(2,1)} %copy-done.1, bf16[8,144,256]{2,1,0:T(8,128)(2,1)} %all_to_all.30.a_ref.e_ref), custom_call_target="tpu_custom_call" | custom-call | flops 1048576 | bytes 3145728 | tf_op jit(solution)/shard_map/finish/pallas_call | solution.py:269
  (1 shorter events, 0.0 us)
Async XLA Ops:
  0.6 93.6 %copy-start = (s32[2,8,128]{2,1,0:T(8,128)S(1)}, s32[2,8,128]{2,1,0:T(8,128)}, u32[]{:S(2)}) copy-start(s32[2,8,128]{2,1,0:T(8,128)} %param.9) | copy-start | bytes 24580
  7.2 14.9 %all-to-all-start.2 = ((bf16[8,256,128]{2,1,0:T(8,128)(2,1)}), bf16[8,256,128]{2,1,0:T(8,128)(2,1)S(1)}, u32[]{:S(2)}, u32[]{:S(2)}) async-start(bf16[8,256,128]{2,1,0:T(8,128)(2,1)} %dft1.1), calls=%async_computation.2 | async-start | bytes 1048576 | tf_op jit(solution)/shard_map/all_to_all | solution.py:301
  22.1 13.7 %all-to-all-start = ((bf16[8,256,128]{2,1,0:T(8,128)(2,1)}), bf16[8,256,128]{2,1,0:T(8,128)(2,1)S(1)}, u32[]{:S(2)}, u32[]{:S(2)}) async-start(bf16[8,256,128]{2,1,0:T(8,128)(2,1)} %dft0.1), calls=%async_computation | async-start | bytes 1048576 | tf_op jit(solution)/shard_map/all_to_all | solution.py:301
  35.8 25.2 %all-to-all-start.3 = ((bf16[16,256,128]{2,1,0:T(8,128)(2,1)}), bf16[16,256,128]{2,1,0:T(8,128)(2,1)S(1)}, u32[]{:S(2)}, u32[]{:S(2)}) async-start(bf16[16,256,128]{2,1,0:T(8,128)(2,1)} %pad_maximum_fusion.1), calls=%async_computation.3 | async-start | bytes 2097152 | tf_op jit(solution)/shard_map/all_to_all | solution.py:303
  61.1 32.5 %copy-start.2 = (bf16[16,256,128]{2,1,0:T(8,128)(2,1)}, bf16[16,256,128]{2,1,0:T(8,128)(2,1)S(1)}, u32[]{:S(2)}) copy-start(bf16[16,256,128]{2,1,0:T(8,128)(2,1)S(1)} %all-to-all-done.3) | copy-start | bytes 3145732
  61.1 33.8 %all-to-all-start.1 = ((bf16[16,256,128]{2,1,0:T(8,128)(2,1)}), bf16[16,256,128]{2,1,0:T(8,128)(2,1)S(1)}, u32[]{:S(2)}, u32[]{:S(2)}) async-start(bf16[16,256,128]{2,1,0:T(8,128)(2,1)} %pad_maximum_fusion), calls=%async_computation.1 | async-start | bytes 2097152 | tf_op jit(solution)/shard_map/all_to_all | solution.py:303
  64.7 28.9 %copy-start.4 = (s32[8]{0:T(128)S(1)}, s32[8]{0:T(128)}, u32[]{:S(2)}) copy-start(s32[8]{0:T(128)} %param.8) | copy-start | bytes 100
  94.8 1.0 copy-start.3
  120.8 15.6 %all-to-all-start.5 = ((bf16[8,128,256]{2,1,0:T(8,128)(2,1)}), bf16[8,128,256]{2,1,0:T(8,128)(2,1)S(1)}, u32[]{:S(2)}, u32[]{:S(2)}) async-start(bf16[8,128,256]{2,1,0:T(8,128)(2,1)} %project2.1), calls=%async_computation.5 | async-start | bytes 1048576 | tf_op jit(solution)/shard_map/all_to_all | solution.py:308
  136.4 15.0 %copy-start.1 = (bf16[8,128,256]{2,1,0:T(8,128)(2,1)}, bf16[8,128,256]{2,1,0:T(8,128)(2,1)S(1)}, u32[]{:S(2)}) copy-start(bf16[8,128,256]{2,1,0:T(8,128)(2,1)S(1)} %all-to-all-done.5.b_ref) | copy-start | bytes 1572868

commit v2 on v1

v2 whole, which is shorter than its diff:
```python
import math

import jax
import jax.numpy as jnp
from jax import lax
from jax.experimental import pallas as pl
from jax.experimental.pallas import tpu as pltpu
from jax.sharding import Mesh
from jax.sharding import PartitionSpec as P


BF = jnp.bfloat16
F32 = jnp.float32
NT = 4096
SLOTS = 4096
TRACE = ("half", "xl", "z")
EIGHT = ("xl", "z")
ROUND = 12582912.0
R2 = math.sqrt(2.0)
VMEM = 62 << 20
EARLY = 1024


def dot(a, b):
    return jnp.dot(a, b, preferred_element_type=F32)


def to_turn(t):
    return t - ((t + ROUND) - ROUND)


def cos_sin(r):
    y = r * r
    s = r * (
        R2 * 3.14159258
        + y * (R2 * -5.16770688 + y * (R2 * 2.55003138 + y * (R2 * -0.59804517 + y * (R2 * 0.07722012))))
    )
    c = R2 * 0.99999995 + y * (
        R2 * -4.93479286 + y * (R2 * 4.05841192 + y * (R2 * -1.33188016 + y * (R2 * 0.2196968)))
    )
    return 1.0 - s * s, s * c


def cos_sin_short(r):
    y = r * r
    s = r * (R2 * 3.14158202 + y * (R2 * -5.16714279 + y * (R2 * 2.541899 + y * (R2 * -0.55463613))))
    c = R2 * 0.9999933 + y * (R2 * -4.93393802 + y * (R2 * 4.04128385 + y * (R2 * -1.22212706)))
    return 1.0 - s * s, s * c


def low_high(v):
    high = v >> 5
    return (v & 31).astype(F32), high.astype(F32)


def wave_rows(w):
    low, high = low_high(w)
    return jnp.concatenate([high * (1 / 32), low * (1 / 32), low * (1 / 1024), jnp.zeros_like(low)], axis=0)


def place_rows(x):
    low, high = low_high(x)
    return jnp.concatenate([low, high, low, jnp.zeros_like(low)], axis=0)


def patch_rows(ref, patch, start, size):
    return jnp.concatenate([ref[c, pl.ds(patch, 1), pl.ds(start, size)] for c in range(4)], axis=0)


def dft(traces):
    half = NT // 2

    def body(x_ref, o_ref):
        f = pl.program_id(0) * 128 + lax.broadcasted_iota(jnp.int32, (64, 128), 1)
        n = lax.broadcasted_iota(jnp.int32, (64, 128), 0)

        def table(step):
            m = (n * f * step) & (NT - 1)
            m = jnp.where(m >= half, m - NT, m)
            return cos_sin(m.astype(F32) * (1.0 / NT))

        c_far, s_far = table(64)
        c_near, s_near = table(1)
        acc = jnp.zeros((512, 256), F32)
        for chunk in range(half // 256):
            rows = []
            for a in range(chunk * 4, chunk * 4 + 4):
                ca, sa = c_far[a : a + 1, :], s_far[a : a + 1, :]
                real = (ca * c_near - sa * s_near).astype(BF)
                imag = (-(sa * c_near) - ca * s_near).astype(BF)
                rows.append(jnp.concatenate([real, imag], axis=1))
            low = x_ref[:, chunk * 256 : (chunk + 1) * 256]
            high = x_ref[:, half + chunk * 256 : half + (chunk + 1) * 256]
            acc = acc + dot(jnp.concatenate([low, high], axis=0), jnp.concatenate(rows, axis=0))
        odd = (lax.broadcasted_iota(jnp.int32, (256, 256), 1) & 1) == 1
        o_ref[0] = jnp.where(odd, acc[:256] - acc[256:], acc[:256] + acc[256:]).astype(BF)

    return pl.pallas_call(
        body,
        grid=(8,),
        out_shape=jax.ShapeDtypeStruct((8, 256, 256), BF),
        in_specs=[pl.BlockSpec((256, NT), lambda i: (0, 0))],
        out_specs=pl.BlockSpec((1, 256, 256), lambda i: (i, 0, 0)),
        compiler_params=pltpu.CompilerParams(vmem_limit_bytes=VMEM),
        cost_estimate=pl.CostEstimate(flops=2 * 256 * NT * 2048, bytes_accessed=3 << 20, transcendentals=0),
        name="dft",
    )(traces)


def make_atoms(waves, places, first, count):
    rows = 256

    def body(w_ref, x_ref, o_ref):
        patch = lax.axis_index("xl") * 4 + lax.axis_index("z")
        start = lax.axis_index("half") * 2048 + first + pl.program_id(0) * rows
        start = pl.multiple_of(start, rows)
        w = jnp.transpose(wave_rows(patch_rows(w_ref, patch, start, rows))).astype(BF)
        x = place_rows(patch_rows(x_ref, patch, 0, SLOTS)).astype(BF)
        for j in range(16):
            c, s = cos_sin_short(to_turn(dot(w, x[:, j * 256 : (j + 1) * 256])))
            o_ref[:, j * 256 : (j + 1) * 256] = c.astype(BF)
            o_ref[:, SLOTS + j * 256 : SLOTS + (j + 1) * 256] = s.astype(BF)

    whole = pl.BlockSpec((4, 8, 4096), lambda i: (0, 0, 0))
    return pl.pallas_call(
        body,
        grid=(count // rows,),
        out_shape=jax.ShapeDtypeStruct((count, 2 * SLOTS), BF),
        in_specs=[whole, whole],
        out_specs=pl.BlockSpec((rows, 2 * SLOTS), lambda i: (i, 0)),
        compiler_params=pltpu.CompilerParams(vmem_limit_bytes=VMEM),
        cost_estimate=pl.CostEstimate(flops=count * (15 << 20), bytes_accessed=count * 16384, transcendentals=0),
        name="atoms",
    )(waves, places)


def chosen_tables(places, waves, chosen, fold):
    size = 512

    def body(fold_ref, x_ref, w_ref, ch_ref, c_ref, s_ref, g_ref, pick_ref):
        patch = lax.axis_index("xl") * 4 + lax.axis_index("z")
        step = pl.program_id(0)

        @pl.when(step == 0)
        def _():
            rows = [w_ref[c, pl.ds(patch, 1), :] for c in range(4)]
            table3 = rows[0] + rows[1] * 1024 + rows[2] * (1 << 20)
            index = jnp.concatenate([ch_ref[t, pl.ds(patch, 1), :] for t in range(2)] * 4, axis=0)
            low, high = index & 127, index >> 7
            found3 = jnp.zeros((8, 128), jnp.int32)
            found1 = jnp.zeros((8, 128), jnp.int32)
            for r in range(32):
                here = high == r
                lanes = slice(r * 128, (r + 1) * 128)
                g3 = jnp.take_along_axis(jnp.broadcast_to(table3[:, lanes], (8, 128)), low, axis=1)
                g1 = jnp.take_along_axis(jnp.broadcast_to(rows[3][:, lanes], (8, 128)), low, axis=1)
                found3 = jnp.where(here, g3, found3)
                found1 = jnp.where(here, g1, found1)
            parts = [found3 & 1023, (found3 >> 10) & 1023, found3 >> 20, found1]
            picked = [jnp.concatenate([v[t : t + 1] for v in parts], axis=0) for t in range(2)]
            pick_ref[...] = wave_rows(jnp.concatenate(picked, axis=1)).astype(BF)
            g_ref[...] = jnp.zeros((16, 128), F32)

        start = pl.multiple_of(step * size, size)
        x = jnp.transpose(place_rows(patch_rows(x_ref, patch, start, size))).astype(BF)
        c, s = cos_sin(to_turn(dot(x, pick_ref[...])))
        c_ref[...] = c
        s_ref[...] = s
        live = (start + lax.broadcasted_iota(jnp.int32, (size, 128), 0)) < fold_ref[patch]
        c0, c1, s0, s1 = c[:, :128], c[:, 128:], s[:, :128], s[:, 128:]
        real = jnp.where(live, c0 * c1 + s0 * s1, 0.0)
        imag = jnp.where(live, s0 * c1 - c0 * s1, 0.0)
        g_ref[:8, :] += jnp.sum(real.reshape(size // 8, 8, 128), axis=0)
        g_ref[8:, :] += jnp.sum(imag.reshape(size // 8, 8, 128), axis=0)

    whole = pl.BlockSpec((4, 8, 4096), lambda i: (0, 0, 0))
    return pl.pallas_call(
        body,
        grid=(SLOTS // size,),
        out_shape=(
            jax.ShapeDtypeStruct((SLOTS, 256), F32),
            jax.ShapeDtypeStruct((SLOTS, 256), F32),
            jax.ShapeDtypeStruct((16, 128), F32),
        ),
        in_specs=[
            pl.BlockSpec(memory_space=pltpu.SMEM),
            whole,
            whole,
            pl.BlockSpec((2, 8, 128), lambda i: (0, 0, 0)),
        ],
        out_specs=(
            pl.BlockSpec((size, 256), lambda i: (i, 0)),
            pl.BlockSpec((size, 256), lambda i: (i, 0)),
            pl.BlockSpec((16, 128), lambda i: (0, 0)),
        ),
        scratch_shapes=[pltpu.VMEM((16, 256), BF)],
        compiler_params=pltpu.CompilerParams(vmem_limit_bytes=VMEM),
        cost_estimate=pl.CostEstimate(flops=4 << 30, bytes_accessed=9 << 20, transcendentals=0),
        name="tables",
    )(fold, places, waves, chosen)


def pursue(received, cosine, sine, cross, fold, atoms):
    size, blocks, tall = 128, 8, 512
    span = SLOTS // blocks
    parts = len(atoms)
    each = 2048 // parts

    def body(fold_ref, g_ref, r_hbm, c_hbm, s_hbm, *rest):
        a_hbm, (o_ref, r_ref, c_ref, s_ref, a_ref, z_ref, sem, a_sem) = rest[:parts], rest[parts:]
        patch = lax.axis_index("xl") * 4 + lax.axis_index("z")
        loads = []
        for j in range(blocks):
            rows = pl.ds(j * span, span)
            trio = [
                pltpu.make_async_copy(src.at[rows, :], dst.at[rows, :], sem.at[j, k])
                for k, (src, dst) in enumerate([(r_hbm, r_ref), (c_hbm, c_ref), (s_hbm, s_ref)])
            ]
            for copy in trio:
                copy.start()
            loads.append(trio)
        streams = []
        for m in range(2048 // tall):
            piece, offset = divmod(m * tall, each)
            copy = pltpu.make_async_copy(
                a_hbm[piece].at[pl.ds(offset, tall), :], a_ref.at[pl.ds(m * tall, tall), :], a_sem.at[m]
            )
            copy.start()
            streams.append(copy)

        count = fold_ref[patch]
        inverse = 1.0 / jnp.full((1, 128), count, jnp.int32).astype(F32)
        zero = jnp.zeros((8, 128), F32)
        row = lax.broadcasted_iota(jnp.int32, (size, 128), 0)

        def fold8(v):
            return jnp.sum(v.reshape(size // 8, 8, 128), axis=0)

        def gather(j, sums):
            start = pl.multiple_of(j * size, size)
            rows = pl.ds(start, size)
            live = row < count - start
            c0, c1 = c_ref[rows, :128], c_ref[rows, 128:]
            s0, s1 = s_ref[rows, :128], s_ref[rows, 128:]
            re = jnp.where(live, r_ref[rows, :128].astype(F32), 0.0)
            im = jnp.where(live, r_ref[rows, 128:].astype(F32), 0.0)
            new = (re * c0 + im * s0, im * c0 - re * s0, re * c1 + im * s1, im * c1 - re * s1)
            return tuple(a + fold8(b) for a, b in zip(sums, new))

        sums = (zero,) * 4
        for j in range(blocks):
            for copy in loads[j]:
                copy.wait()
            sums = lax.fori_loop(j * span // size, (j + 1) * span // size, gather, sums)
        r0, i0, r1, i1 = [jnp.sum(v, axis=0, keepdims=True) for v in sums]
        gr = jnp.sum(g_ref[:8, :], axis=0, keepdims=True)
        gi = jnp.sum(g_ref[8:, :], axis=0, keepdims=True)
        a0, b0 = r0 * inverse, i0 * inverse
        a1 = (r1 - (a0 * gr - b0 * gi)) * inverse
        b1 = (i1 - (a0 * gi + b0 * gr)) * inverse

        def split(v):
            first = v.astype(BF).astype(F32)
            second = (v - first).astype(BF).astype(F32)
            return [first, second, v - first - second]

        packed = [jnp.concatenate(pair, axis=1) for pair in zip(split(a0), split(b0))]
        packed += [jnp.concatenate(pair, axis=1) for pair in zip(split(a1), split(b1))]
        packed = jnp.concatenate(packed + [jnp.zeros((10, 256), F32)], axis=0).astype(BF)
        for b in range(8):
            o_ref[b, 256:, :] = packed

        def subtract(j, carry):
            start = pl.multiple_of(j * size, size)
            rows = pl.ds(start, size)
            live = row < count - start
            c0, c1 = c_ref[rows, :128], c_ref[rows, 128:]
            s0, s1 = s_ref[rows, :128], s_ref[rows, 128:]
            re = r_ref[rows, :128].astype(F32) - (a0 * c0 - b0 * s0) - (a1 * c1 - b1 * s1)
            im = r_ref[rows, 128:].astype(F32) - (a0 * s0 + b0 * c0) - (a1 * s1 + b1 * c1)
            re = jnp.where(live, re, 0.0).astype(BF)
            im = jnp.where(live, im, 0.0).astype(BF)
            z_ref[0, rows, :128] = re
            z_ref[0, rows, 128:] = im
            z_ref[1, rows, :128] = im
            z_ref[1, rows, 128:] = -re
            return carry

        lax.fori_loop(0, SLOTS // size, subtract, 0)

        for m in range(2048 // tall):
            streams[m].wait()
            rows = pl.ds(m * tall, tall)
            acc = dot(a_ref[rows, :SLOTS], z_ref[0]) + dot(a_ref[rows, SLOTS:], z_ref[1])
            for b in range(tall // 256):
                o_ref[m * (tall // 256) + b, :256, :] = acc[b * 256 : (b + 1) * 256].astype(BF)

    hbm = pl.BlockSpec(memory_space=pl.ANY)
    whole = pl.BlockSpec(memory_space=pltpu.VMEM)
    return pl.pallas_call(
        body,
        out_shape=jax.ShapeDtypeStruct((8, 272, 256), BF),
        in_specs=[pl.BlockSpec(memory_space=pltpu.SMEM), whole] + [hbm] * (3 + parts),
        out_specs=whole,
        scratch_shapes=[
            pltpu.VMEM((SLOTS, 256), BF),
            pltpu.VMEM((SLOTS, 256), F32),
            pltpu.VMEM((SLOTS, 256), F32),
            pltpu.VMEM((2048, 2 * SLOTS), BF),
            pltpu.VMEM((2, SLOTS, 256), BF),
            pltpu.SemaphoreType.DMA((blocks, 3)),
            pltpu.SemaphoreType.DMA((2048 // tall,)),
        ],
        compiler_params=pltpu.CompilerParams(vmem_limit_bytes=VMEM),
        cost_estimate=pl.CostEstimate(flops=9 << 30, bytes_accessed=45 << 20, transcendentals=0),
        name="pursue",
    )(fold, cross, received, cosine, sine, *atoms)


def finish(moved):
    step = 64

    def body(a_ref, e_ref, o_ref, c_ref):
        for p in range(8):
            for part in range(2):
                lanes = pl.ds(part * 128, 128)
                o_ref[pl.ds(2 * p + part, step, stride=16), :] = a_ref[p, :, lanes].astype(F32)

        @pl.when(pl.program_id(0) == 0)
        def _():
            for p in range(8):
                v = e_ref[p].astype(F32)
                for t in range(2):
                    total = v[3 * t : 3 * t + 1] + (v[3 * t + 1 : 3 * t + 2] + v[3 * t + 2 : 3 * t + 3])
                    row = t * 16 + 2 * p
                    c_ref[row : row + 1, :] = total[:, :128]
                    c_ref[row + 1 : row + 2, :] = total[:, 128:]

    return pl.pallas_call(
        body,
        grid=(256 // step,),
        out_shape=(jax.ShapeDtypeStruct((4096, 128), F32), jax.ShapeDtypeStruct((32, 128), F32)),
        in_specs=[
            pl.BlockSpec((8, step, 256), lambda i: (0, i, 0)),
            pl.BlockSpec((8, 16, 256), lambda i: (0, 16, 0)),
        ],
        out_specs=(
            pl.BlockSpec((step * 16, 128), lambda i: (i, 0)),
            pl.BlockSpec((32, 128), lambda i: (0, 0)),
        ),
        compiler_params=pltpu.CompilerParams(vmem_limit_bytes=VMEM),
        cost_estimate=pl.CostEstimate(flops=1 << 20, bytes_accessed=3 << 20, transcendentals=0),
        name="finish",
    )(moved, moved)


def local(traces, coords, wavenumbers, fold, selected):
    sent = dft(traces[0])
    moved = lax.all_to_all(sent, "freq", split_axis=0, concat_axis=0, tiled=True)
    both = jnp.concatenate([moved, moved], axis=0)
    moved = lax.all_to_all(both, TRACE, split_axis=0, concat_axis=0, tiled=True)
    early = make_atoms(wavenumbers, coords, 0, EARLY)
    late = make_atoms(wavenumbers, coords, EARLY, 2048 - EARLY)
    cosine, sine, cross = chosen_tables(coords, wavenumbers, selected, fold)
    sent = pursue(moved.reshape(SLOTS, 256), cosine, sine, cross, fold, [early, late])
    moved = lax.all_to_all(sent, EIGHT, split_axis=0, concat_axis=0, tiled=True)
    spectrum, coefficients = finish(moved)
    return spectrum.reshape(256, 8, 2, 128), coefficients.reshape(2, 8, 2, 128)


def solution(mesh):
    split = Mesh(mesh.devices.reshape(8, 2, 2, 4), ("freq",) + TRACE)
    return jax.shard_map(
        local,
        mesh=split,
        in_specs=(P("freq", TRACE, None), P(), P(), P(), P(None, None, "freq")),
        out_specs=(P(TRACE, None, None, "freq"), P(None, None, None, "freq")),
        check_vma=False,
    )
```

time: 156 us -> 140 us (0.90)
  blocking collectives: 15 us -> 41.8 us
  waiting for transfers between devices: 25.3 us -> 0.01 us
  starting transfers between devices: 25.1 us -> 7.93 us
  Pallas kernels: 80.6 us -> 87.5 us
  local copies, waits for them, and re-layouts: 6.52 us -> 0 us
    all_to_all x1 -> x2, blocking collectives: 15 us -> 41.8 us  [the longest x1 21.3 us: local(): moved = lax.all_to_all(sent, EIGHT, split_axis=0, concat_axis=0, tiled=True)]
    all_to_all x3 -> x0, starting transfers between devices: 13.6 us -> none  [the longest x2 8.08 us: local(): lax.all_to_all(sent, 'freq', split_axis=0, concat_axis=0, tiled=True)]
    all_to_all x3 -> x0, waiting for transfers between devices: 13.4 us -> none  [the longest x2 13.4 us: local(): lax.all_to_all(sent, 'freq', split_axis=0, concat_axis=0, tiled=True)]
    all_to_all x2 -> x1, waiting for transfers between devices: 11.9 us -> 0.01 us  [local(): moved = lax.all_to_all(both, TRACE, split_axis=0, concat_axis=0, tiled=True)]
    dynamic_slice x4 -> x0, local copies, waits for them, and re-layouts: 4.25 us -> none  [the longest x1 1.91 us: local(): waves = lax.dynamic_slice_in_dim(wavenumbers, patch, 1, 1)[:, 0]]
    pallas_call x1 -> x2, Pallas kernels: 28.8 us -> 32.6 us  [make_atoms(): pl.pallas_call(body, grid=(count // rows,), out_shape=jax.ShapeDtypeStruc...]
    all_to_all x2 -> x1, starting transfers between devices: 11.5 us -> 7.93 us  [local(): moved = lax.all_to_all(both, TRACE, split_axis=0, concat_axis=0, tiled=True)]
    pallas_call x6 -> x4, Pallas kernels: 51.8 us -> 54.9 us  [the longest x1 33.2 us: pursue(): pl.pallas_call(body, out_shape=jax.ShapeDtypeStruct((8, 272, 256), BF), i...]
  transfers between devices with their start and end apart: 5 -> 1, of which waited for: 3 -> 0; matrix products, arithmetic and copies ran while one was open for 5% -> 0% of each run, Pallas kernels for 29% -> 30%
where the time goes in v2:
time: 140 us; the launch traced here: 139 us
  Pallas kernels  87.5 us (62%)
  blocking collectives  41.8 us (30%)
  starting transfers between devices  7.93 us (6%)
  other arithmetic  1.5 us (1%)
    pallas_call x1, Pallas kernels, pursue(): pl.pallas_call(body, out_shape=jax.ShapeDtypeStruct((8, 272, 256), BF), i...  33.2 us
    pallas_call x2, Pallas kernels, make_atoms(): pl.pallas_call(body, grid=(count // rows,), out_shape=jax.ShapeDtypeStruc...  32.6 us
    all_to_all x1, blocking collectives, local(): moved = lax.all_to_all(sent, EIGHT, split_axis=0, concat_axis=0, tiled=True)  21.3 us
    all_to_all x1, blocking collectives, local(): lax.all_to_all(sent, 'freq', split_axis=0, concat_axis=0, tiled=True)  20.6 us
    pallas_call x1, Pallas kernels, chosen_tables(): pl.pallas_call(body, grid=(SLOTS // size,), out_shape=(jax.ShapeDtypeStru...  8.95 us
    pallas_call x1, Pallas kernels, dft(): pl.pallas_call(body, grid=(8,), out_shape=jax.ShapeDtypeStruct((8, 256, 2...  8.72 us
    all_to_all x1, starting transfers between devices, local(): moved = lax.all_to_all(both, TRACE, split_axis=0, concat_axis=0, tiled=True)  7.93 us
    pallas_call x1, Pallas kernels, finish(): pl.pallas_call(body, grid=(256 // step,), out_shape=(jax.ShapeDtypeStruct...  4.01 us
  transfers between devices with their start and end apart: 1, of which 0 were waited for; matrix products, arithmetic and copies ran while one was open for 0% of the time, Pallas kernels for 30%

profile of v2, /device:TPU:0, one launch (start us, length us, event | category | flops | bytes accessed | tf_op | source)
XLA Modules:
  0.0 139.4 jit_solution(5634743709668881076)
XLA Ops:
  0.6 8.7 %dft.1 = bf16[8,256,256]{2,1,0:T(8,128)(2,1)} custom-call(bf16[256,4096]{1,0:T(8,128)(2,1)} %bitcast.4), custom_call_target="tpu_custom_call" | custom-call | flops 4294967296 | bytes 3145728 | tf_op jit(solution)/shard_map/dft/pallas_call | solution.py:98
  9.4 20.6 %all_to_all.15 = bf16[8,256,256]{2,1,0:T(8,128)(2,1)S(1)} all-to-all(bf16[8,256,256]{2,1,0:T(8,128)(2,1)} %dft.1), channel_id=1, replica_groups=mesh['freq'=8,'half'=2,'xl'=2,'z'=4] {'freq'}, dimensions={0} | all-to-all | bytes 2097152 | tf_op jit(solution)/shard_map/all_to_all | solution.py:359
  29.9 1.5 %pad_maximum_fusion = bf16[16,256,256]{2,1,0:T(8,128)(2,1)} fusion(bf16[8,256,256]{2,1,0:T(8,128)(2,1)S(1)} %all_to_all.15), kind=kLoop, calls=%fused_computation | loop fusion | flops 1048576 | bytes 3145728 | tf_op jit(solution)/shard_map/concatenate | solution.py:360
  31.4 7.9 %all-to-all-start.1 = ((bf16[16,256,256]{2,1,0:T(8,128)(2,1)}), bf16[16,256,256]{2,1,0:T(8,128)(2,1)}, u32[]{:S(2)}, u32[]{:S(2)}) async-start(bf16[16,256,256]{2,1,0:T(8,128)(2,1)} %pad_maximum_fusion), calls=%async_computation.1 | async-start | bytes 4194304 | tf_op jit(solution)/shard_map/all_to_all | solution.py:361
  39.3 16.3 %atoms.3.rest_1_ = bf16[1024,8192]{1,0:T(8,128)(2,1)} custom-call(s32[4,8,4096]{2,1,0:T(8,128)} %w_ref.5, s32[4,8,4096]{2,1,0:T(8,128)} %x_ref.5), custom_call_target="tpu_custom_call" | custom-call | flops 16106127360 | bytes 16777216 | tf_op jit(solution)/shard_map/atoms/pallas_call | solution.py:125
  55.6 8.9 %tables.1 = (f32[4096,256]{1,0:T(8,128)}, f32[4096,256]{1,0:T(8,128)}, f32[16,128]{1,0:T(8,128)}) custom-call(s32[8]{0:T(128)} %fold_ref.3, s32[4,8,4096]{2,1,0:T(8,128)} %x_ref.5, s32[4,8,4096]{2,1,0:T(8,128)} %w_ref.5, s32[2,8,128]{2,1,0:T(8,128)} %ch_ref.1), custom_call_target="tpu_custom_call" | custom-call | flops 4294967296 | bytes 9437184 | tf_op jit(solution)/shard_map/tables/pallas_call | solution.py:177
  64.6 16.3 %atoms.2.rest_0_ = bf16[1024,8192]{1,0:T(8,128)(2,1)} custom-call(s32[4,8,4096]{2,1,0:T(8,128)} %w_ref.5, s32[4,8,4096]{2,1,0:T(8,128)} %x_ref.5), custom_call_target="tpu_custom_call" | custom-call | flops 16106127360 | bytes 16777216 | tf_op jit(solution)/shard_map/atoms/pallas_call | solution.py:125
  80.8 0.0 all-to-all-done.1
  80.9 33.2 %pursue.1 = bf16[8,272,256]{2,1,0:T(8,128)(2,1)} custom-call(s32[8]{0:T(128)} %fold_ref.3, f32[16,128]{1,0:T(8,128)} %get-tuple-element.7.g_ref, bf16[4096,256]{1,0:T(8,128)(2,1)} %bitcast.1.r_hbm, f32[4096,256]{1,0:T(8,128)} %get-tuple-element.8.c_hbm, f32[4096,256]{1,0:T(8,128)} %get-tuple-element.9.s_hbm, bf16[1024,8192]{1,0:T(8,128)(2,1)} %atoms.2.rest_0_, ...), custom_call_target="tpu_custom_call" | custom-call | flops 9663676416 | bytes 47185920 | tf_op jit(solution)/shard_map/pursue/pallas_call | solution.py:300
  114.1 21.3 %all_to_all.16.a_ref.e_ref = bf16[8,272,256]{2,1,0:T(8,128)(2,1)} all-to-all(bf16[8,272,256]{2,1,0:T(8,128)(2,1)} %pursue.1), channel_id=1, replica_groups=mesh['freq'=8,'half'=2,'xl'=2,'z'=4] {'xl','z'}, dimensions={0} | all-to-all | bytes 2228224 | tf_op jit(solution)/shard_map/all_to_all | solution.py:366
  135.4 4.0 %finish.1 = (f32[4096,128]{1,0:T(8,128)}, f32[32,128]{1,0:T(8,128)}) custom-call(bf16[8,272,256]{2,1,0:T(8,128)(2,1)} %all_to_all.16.a_ref.e_ref, bf16[8,272,256]{2,1,0:T(8,128)(2,1)} %all_to_all.16.a_ref.e_ref), custom_call_target="tpu_custom_call" | custom-call | flops 1048576 | bytes 3145728 | tf_op jit(solution)/shard_map/finish/pallas_call | solution.py:339
Async XLA Ops:
  31.4 49.4 %all-to-all-start.1 = ((bf16[16,256,256]{2,1,0:T(8,128)(2,1)}), bf16[16,256,256]{2,1,0:T(8,128)(2,1)}, u32[]{:S(2)}, u32[]{:S(2)}) async-start(bf16[16,256,256]{2,1,0:T(8,128)(2,1)} %pad_maximum_fusion), calls=%async_computation.1 | async-start | bytes 4194304 | tf_op jit(solution)/shard_map/all_to_all | solution.py:361

commit v3 on v2

--- a/solution.py
+++ b/solution.py
@@ -69,10 +69,11 @@
 
 def dft(traces):
     half = NT // 2
+    width = 256
 
     def body(x_ref, o_ref):
-        f = pl.program_id(0) * 128 + lax.broadcasted_iota(jnp.int32, (64, 128), 1)
-        n = lax.broadcasted_iota(jnp.int32, (64, 128), 0)
+        f = pl.program_id(0) * width + lax.broadcasted_iota(jnp.int32, (64, width), 1)
+        n = lax.broadcasted_iota(jnp.int32, (64, width), 0)
 
         def table(step):
             m = (n * f * step) & (NT - 1)
@@ -81,7 +82,7 @@
 
         c_far, s_far = table(64)
         c_near, s_near = table(1)
-        acc = jnp.zeros((512, 256), F32)
+        acc = jnp.zeros((512, 2 * width), F32)
         for chunk in range(half // 256):
             rows = []
             for a in range(chunk * 4, chunk * 4 + 4):
@@ -92,15 +93,19 @@
             low = x_ref[:, chunk * 256 : (chunk + 1) * 256]
             high = x_ref[:, half + chunk * 256 : half + (chunk + 1) * 256]
             acc = acc + dot(jnp.concatenate([low, high], axis=0), jnp.concatenate(rows, axis=0))
-        odd = (lax.broadcasted_iota(jnp.int32, (256, 256), 1) & 1) == 1
-        o_ref[0] = jnp.where(odd, acc[:256] - acc[256:], acc[:256] + acc[256:]).astype(BF)
+        odd = (lax.broadcasted_iota(jnp.int32, (256, 2 * width), 1) & 1) == 1
+        both = jnp.where(odd, acc[:256] - acc[256:], acc[:256] + acc[256:]).astype(BF)
+        for g in range(width // 128):
+            lanes = slice(g * 128, (g + 1) * 128)
+            o_ref[g, :, :128] = both[:, :width][:, lanes]
+            o_ref[g, :, 128:] = both[:, width:][:, lanes]
 
     return pl.pallas_call(
         body,
-        grid=(8,),
+        grid=(1024 // width,),
         out_shape=jax.ShapeDtypeStruct((8, 256, 256), BF),
         in_specs=[pl.BlockSpec((256, NT), lambda i: (0, 0))],
-        out_specs=pl.BlockSpec((1, 256, 256), lambda i: (i, 0, 0)),
+        out_specs=pl.BlockSpec((width // 128, 256, 256), lambda i: (i, 0, 0)),
         compiler_params=pltpu.CompilerParams(vmem_limit_bytes=VMEM),
         cost_estimate=pl.CostEstimate(flops=2 * 256 * NT * 2048, bytes_accessed=3 << 20, transcendentals=0),
         name="dft",
@@ -110,14 +115,18 @@
 def make_atoms(waves, places, first, count):
     rows = 256
 
-    def body(w_ref, x_ref, o_ref):
+    def body(w_ref, x_ref, o_ref, place_ref):
         patch = lax.axis_index("xl") * 4 + lax.axis_index("z")
+
+        @pl.when(pl.program_id(0) == 0)
+        def _():
+            place_ref[...] = place_rows(patch_rows(x_ref, patch, 0, SLOTS)).astype(BF)
+
         start = lax.axis_index("half") * 2048 + first + pl.program_id(0) * rows
         start = pl.multiple_of(start, rows)
         w = jnp.transpose(wave_rows(patch_rows(w_ref, patch, start, rows))).astype(BF)
-        x = place_rows(patch_rows(x_ref, patch, 0, SLOTS)).astype(BF)
         for j in range(16):
-            c, s = cos_sin_short(to_turn(dot(w, x[:, j * 256 : (j + 1) * 256])))
+            c, s = cos_sin_short(to_turn(dot(w, place_ref[:, j * 256 : (j + 1) * 256])))
             o_ref[:, j * 256 : (j + 1) * 256] = c.astype(BF)
             o_ref[:, SLOTS + j * 256 : SLOTS + (j + 1) * 256] = s.astype(BF)
 
@@ -128,6 +137,7 @@
         out_shape=jax.ShapeDtypeStruct((count, 2 * SLOTS), BF),
         in_specs=[whole, whole],
         out_specs=pl.BlockSpec((rows, 2 * SLOTS), lambda i: (i, 0)),
+        scratch_shapes=[pltpu.VMEM((16, SLOTS), BF)],
         compiler_params=pltpu.CompilerParams(vmem_limit_bytes=VMEM),
         cost_estimate=pl.CostEstimate(flops=count * (15 << 20), bytes_accessed=count * 16384, transcendentals=0),
         name="atoms",
@@ -201,7 +211,7 @@
 
 
 def pursue(received, cosine, sine, cross, fold, atoms):
-    size, blocks, tall = 128, 8, 512
+    size, blocks, tall, ahead = 128, 8, 256, 3
     span = SLOTS // blocks
     parts = len(atoms)
     each = 2048 // parts
@@ -212,21 +222,21 @@
         loads = []
         for j in range(blocks):
             rows = pl.ds(j * span, span)
-            trio = [
-                pltpu.make_async_copy(src.at[rows, :], dst.at[rows, :], sem.at[j, k])
-                for k, (src, dst) in enumerate([(r_hbm, r_ref), (c_hbm, c_ref), (s_hbm, s_ref)])
-            ]
-            for copy in trio:
+            loads.append(
+                [
+                    pltpu.make_async_copy(src.at[rows, :], dst.at[rows, :], sem.at[j, k])
+                    for k, (src, dst) in enumerate([(r_hbm, r_ref), (c_hbm, c_ref), (s_hbm, s_ref)])
+                ]
+            )
+        for j in range(3):
+            for copy in loads[j]:
                 copy.start()
-            loads.append(trio)
-        streams = []
-        for m in range(2048 // tall):
+
+        def stream(m):
             piece, offset = divmod(m * tall, each)
-            copy = pltpu.make_async_copy(
+            return pltpu.make_async_copy(
                 a_hbm[piece].at[pl.ds(offset, tall), :], a_ref.at[pl.ds(m * tall, tall), :], a_sem.at[m]
             )
-            copy.start()
-            streams.append(copy)
 
         count = fold_ref[patch]
         inverse = 1.0 / jnp.full((1, 128), count, jnp.int32).astype(F32)
@@ -251,6 +261,11 @@
         for j in range(blocks):
             for copy in loads[j]:
                 copy.wait()
+            if j + 3 < blocks:
+                for copy in loads[j + 3]:
+                    copy.start()
+            elif j + 3 < blocks + ahead:
+                stream(j + 3 - blocks).start()
             sums = lax.fori_loop(j * span // size, (j + 1) * span // size, gather, sums)
         r0, i0, r1, i1 = [jnp.sum(v, axis=0, keepdims=True) for v in sums]
         gr = jnp.sum(g_ref[:8, :], axis=0, keepdims=True)
@@ -288,12 +303,20 @@
 
         lax.fori_loop(0, SLOTS // size, subtract, 0)
 
-        for m in range(2048 // tall):
-            streams[m].wait()
-            rows = pl.ds(m * tall, tall)
+        def project(m, carry):
+            rows = pl.ds(pl.multiple_of(m * tall, tall), tall)
+            pltpu.make_async_copy(a_ref.at[rows, :], a_ref.at[rows, :], a_sem.at[m]).wait()
+            for later in range(ahead, 2048 // tall):
+
+                @pl.when(m == later - ahead)
+                def _(later=later):
+                    stream(later).start()
+
             acc = dot(a_ref[rows, :SLOTS], z_ref[0]) + dot(a_ref[rows, SLOTS:], z_ref[1])
-            for b in range(tall // 256):
-                o_ref[m * (tall // 256) + b, :256, :] = acc[b * 256 : (b + 1) * 256].astype(BF)
+            o_ref[m, :256, :] = acc.astype(BF)
+            return carry
+
+        lax.fori_loop(0, 2048 // tall, project, 0)
 
     hbm = pl.BlockSpec(memory_space=pl.ANY)
     whole = pl.BlockSpec(memory_space=pltpu.VMEM)

time: 140 us -> 124 us (0.89)
  Pallas kernels: 87.5 us -> 71.7 us
    pallas_call x1, Pallas kernels: 33.2 us -> 18.7 us  [pursue(): pl.pallas_call(body, out_shape=jax.ShapeDtypeStruct((8, 272, 256), BF), i...]
  transfers between devices with their start and end apart: 1 -> 1, of which waited for: 0 -> 0; matrix products, arithmetic and copies ran while one was open for 0% -> 0% of each run, Pallas kernels for 30% -> 33%
where the time goes in v3:
time: 124 us
  Pallas kernels  71.7 us (58%)
  blocking collectives  41.8 us (34%)
  starting transfers between devices  7.92 us (6%)
  other arithmetic  1.5 us (1%)
    pallas_call x2, Pallas kernels, make_atoms(): pl.pallas_call(body, grid=(count // rows,), out_shape=jax.ShapeDtypeStruc...  32.2 us
    all_to_all x1, blocking collectives, local(): moved = lax.all_to_all(sent, EIGHT, split_axis=0, concat_axis=0, tiled=True)  21.3 us
    all_to_all x1, blocking collectives, local(): lax.all_to_all(sent, 'freq', split_axis=0, concat_axis=0, tiled=True)  20.6 us
    pallas_call x1, Pallas kernels, pursue(): pl.pallas_call(body, out_shape=jax.ShapeDtypeStruct((8, 272, 256), BF), i...  18.7 us
    pallas_call x1, Pallas kernels, chosen_tables(): pl.pallas_call(body, grid=(SLOTS // size,), out_shape=(jax.ShapeDtypeStru...  8.95 us
    all_to_all x1, starting transfers between devices, local(): moved = lax.all_to_all(both, TRACE, split_axis=0, concat_axis=0, tiled=True)  7.92 us
    pallas_call x1, Pallas kernels, dft(): pl.pallas_call(body, grid=(1024 // width,), out_shape=jax.ShapeDtypeStruc...  7.83 us
    pallas_call x1, Pallas kernels, finish(): pl.pallas_call(body, grid=(256 // step,), out_shape=(jax.ShapeDtypeStruct...  4.01 us
  transfers between devices with their start and end apart: 1, of which 0 were waited for; matrix products, arithmetic and copies ran while one was open for 0% of the time, Pallas kernels for 33%

profile of v3, /device:TPU:0, one launch (start us, length us, event | category | flops | bytes accessed | tf_op | source)
XLA Modules:
  0.0 123.6 jit_solution(8309266448001954072)
XLA Ops:
  0.6 7.8 %dft.1 = bf16[8,256,256]{2,1,0:T(8,128)(2,1)} custom-call(bf16[256,4096]{1,0:T(8,128)(2,1)} %bitcast.4), custom_call_target="tpu_custom_call" | custom-call | flops 4294967296 | bytes 3145728 | tf_op jit(solution)/shard_map/dft/pallas_call | solution.py:103
  8.5 20.6 %all_to_all.15 = bf16[8,256,256]{2,1,0:T(8,128)(2,1)S(1)} all-to-all(bf16[8,256,256]{2,1,0:T(8,128)(2,1)} %dft.1), channel_id=1, replica_groups=mesh['freq'=8,'half'=2,'xl'=2,'z'=4] {'freq'}, dimensions={0} | all-to-all | bytes 2097152 | tf_op jit(solution)/shard_map/all_to_all | solution.py:382
  29.0 1.5 %pad_maximum_fusion = bf16[16,256,256]{2,1,0:T(8,128)(2,1)} fusion(bf16[8,256,256]{2,1,0:T(8,128)(2,1)S(1)} %all_to_all.15), kind=kLoop, calls=%fused_computation | loop fusion | flops 1048576 | bytes 3145728 | tf_op jit(solution)/shard_map/concatenate | solution.py:383
  30.5 7.9 %all-to-all-start.1 = ((bf16[16,256,256]{2,1,0:T(8,128)(2,1)}), bf16[16,256,256]{2,1,0:T(8,128)(2,1)}, u32[]{:S(2)}, u32[]{:S(2)}) async-start(bf16[16,256,256]{2,1,0:T(8,128)(2,1)} %pad_maximum_fusion), calls=%async_computation.1 | async-start | bytes 4194304 | tf_op jit(solution)/shard_map/all_to_all | solution.py:384
  38.4 16.1 %atoms.3.rest_1_ = bf16[1024,8192]{1,0:T(8,128)(2,1)} custom-call(s32[4,8,4096]{2,1,0:T(8,128)} %w_ref.5, s32[4,8,4096]{2,1,0:T(8,128)} %x_ref.5), custom_call_target="tpu_custom_call" | custom-call | flops 16106127360 | bytes 16777216 | tf_op jit(solution)/shard_map/atoms/pallas_call | solution.py:134
  54.6 8.9 %tables.1 = (f32[4096,256]{1,0:T(8,128)}, f32[4096,256]{1,0:T(8,128)}, f32[16,128]{1,0:T(8,128)}) custom-call(s32[8]{0:T(128)} %fold_ref.3, s32[4,8,4096]{2,1,0:T(8,128)} %x_ref.5, s32[4,8,4096]{2,1,0:T(8,128)} %w_ref.5, s32[2,8,128]{2,1,0:T(8,128)} %ch_ref.1), custom_call_target="tpu_custom_call" | custom-call | flops 4294967296 | bytes 9437184 | tf_op jit(solution)/shard_map/tables/pallas_call | solution.py:187
  63.5 16.1 %atoms.2.rest_0_ = bf16[1024,8192]{1,0:T(8,128)(2,1)} custom-call(s32[4,8,4096]{2,1,0:T(8,128)} %w_ref.5, s32[4,8,4096]{2,1,0:T(8,128)} %x_ref.5), custom_call_target="tpu_custom_call" | custom-call | flops 16106127360 | bytes 16777216 | tf_op jit(solution)/shard_map/atoms/pallas_call | solution.py:134
  79.6 0.0 all-to-all-done.1
  79.6 18.7 %pursue.1 = bf16[8,272,256]{2,1,0:T(8,128)(2,1)} custom-call(s32[8]{0:T(128)} %fold_ref.3, f32[16,128]{1,0:T(8,128)} %get-tuple-element.7.g_ref, bf16[4096,256]{1,0:T(8,128)(2,1)} %bitcast.1.r_hbm, f32[4096,256]{1,0:T(8,128)} %get-tuple-element.8.c_hbm, f32[4096,256]{1,0:T(8,128)} %get-tuple-element.9.s_hbm, bf16[1024,8192]{1,0:T(8,128)(2,1)} %atoms.2.rest_0_, ...), custom_call_target="tpu_custom_call" | custom-call | flops 9663676416 | bytes 47185920 | tf_op jit(solution)/shard_map/pursue/pallas_call | solution.py:323
  98.3 21.3 %all_to_all.16.a_ref.e_ref = bf16[8,272,256]{2,1,0:T(8,128)(2,1)} all-to-all(bf16[8,272,256]{2,1,0:T(8,128)(2,1)} %pursue.1), channel_id=1, replica_groups=mesh['freq'=8,'half'=2,'xl'=2,'z'=4] {'xl','z'}, dimensions={0} | all-to-all | bytes 2228224 | tf_op jit(solution)/shard_map/all_to_all | solution.py:389
  119.6 4.0 %finish.1 = (f32[4096,128]{1,0:T(8,128)}, f32[32,128]{1,0:T(8,128)}) custom-call(bf16[8,272,256]{2,1,0:T(8,128)(2,1)} %all_to_all.16.a_ref.e_ref, bf16[8,272,256]{2,1,0:T(8,128)(2,1)} %all_to_all.16.a_ref.e_ref), custom_call_target="tpu_custom_call" | custom-call | flops 1048576 | bytes 3145728 | tf_op jit(solution)/shard_map/finish/pallas_call | solution.py:362
Async XLA Ops:
  30.5 49.1 %all-to-all-start.1 = ((bf16[16,256,256]{2,1,0:T(8,128)(2,1)}), bf16[16,256,256]{2,1,0:T(8,128)(2,1)}, u32[]{:S(2)}, u32[]{:S(2)}) async-start(bf16[16,256,256]{2,1,0:T(8,128)(2,1)} %pad_maximum_fusion), calls=%async_computation.1 | async-start | bytes 4194304 | tf_op jit(solution)/shard_map/all_to_all | solution.py:384

commit v4 on v3

--- a/solution.py
+++ b/solution.py
@@ -18,7 +18,7 @@
 ROUND = 12582912.0
 R2 = math.sqrt(2.0)
 VMEM = 62 << 20
-EARLY = 1024
+EARLY = 896
 
 
 def dot(a, b):
@@ -43,9 +43,9 @@
 
 def cos_sin_short(r):
     y = r * r
-    s = r * (R2 * 3.14158202 + y * (R2 * -5.16714279 + y * (R2 * 2.541899 + y * (R2 * -0.55463613))))
+    s = r * (R2 * 3.14064003 + y * (R2 * -5.13690521 + y * (R2 * 2.29954682)))
     c = R2 * 0.9999933 + y * (R2 * -4.93393802 + y * (R2 * 4.04128385 + y * (R2 * -1.22212706)))
-    return 1.0 - s * s, s * c
+    return c * c - 1.0, s * c
 
 
 def low_high(v):
@@ -113,18 +113,19 @@
 
 
 def make_atoms(waves, places, first, count):
-    rows = 256
-
-    def body(w_ref, x_ref, o_ref, place_ref):
+    rows = 128
+
+    def body(w_ref, x_ref, o_ref, place_ref, wave_ref):
         patch = lax.axis_index("xl") * 4 + lax.axis_index("z")
 
         @pl.when(pl.program_id(0) == 0)
         def _():
             place_ref[...] = place_rows(patch_rows(x_ref, patch, 0, SLOTS)).astype(BF)
+            wave_ref[...] = wave_rows(patch_rows(w_ref, patch, 0, 4096))
 
         start = lax.axis_index("half") * 2048 + first + pl.program_id(0) * rows
         start = pl.multiple_of(start, rows)
-        w = jnp.transpose(wave_rows(patch_rows(w_ref, patch, start, rows))).astype(BF)
+        w = jnp.transpose(wave_ref[:, pl.ds(start, rows)]).astype(BF)
         for j in range(16):
             c, s = cos_sin_short(to_turn(dot(w, place_ref[:, j * 256 : (j + 1) * 256])))
             o_ref[:, j * 256 : (j + 1) * 256] = c.astype(BF)
@@ -137,7 +138,7 @@
         out_shape=jax.ShapeDtypeStruct((count, 2 * SLOTS), BF),
         in_specs=[whole, whole],
         out_specs=pl.BlockSpec((rows, 2 * SLOTS), lambda i: (i, 0)),
-        scratch_shapes=[pltpu.VMEM((16, SLOTS), BF)],
+        scratch_shapes=[pltpu.VMEM((16, SLOTS), BF), pltpu.VMEM((16, 4096), F32)],
         compiler_params=pltpu.CompilerParams(vmem_limit_bytes=VMEM),
         cost_estimate=pl.CostEstimate(flops=count * (15 << 20), bytes_accessed=count * 16384, transcendentals=0),
         name="atoms",
@@ -214,7 +215,6 @@
     size, blocks, tall, ahead = 128, 8, 256, 3
     span = SLOTS // blocks
     parts = len(atoms)
-    each = 2048 // parts
 
     def body(fold_ref, g_ref, r_hbm, c_hbm, s_hbm, *rest):
         a_hbm, (o_ref, r_ref, c_ref, s_ref, a_ref, z_ref, sem, a_sem) = rest[:parts], rest[parts:]
@@ -233,10 +233,14 @@
                 copy.start()
 
         def stream(m):
-            piece, offset = divmod(m * tall, each)
-            return pltpu.make_async_copy(
-                a_hbm[piece].at[pl.ds(offset, tall), :], a_ref.at[pl.ds(m * tall, tall), :], a_sem.at[m]
-            )
+            for k, (low, high) in enumerate([(0, EARLY), (EARLY, 2048)]):
+                first, last = max(m * tall, low), min((m + 1) * tall, high)
+                if first < last:
+                    pltpu.make_async_copy(
+                        a_hbm[k].at[pl.ds(first - low, last - first), :],
+                        a_ref.at[pl.ds(first, last - first), :],
+                        a_sem.at[m],
+                    ).start()
 
         count = fold_ref[patch]
         inverse = 1.0 / jnp.full((1, 128), count, jnp.int32).astype(F32)
@@ -265,7 +269,7 @@
                 for copy in loads[j + 3]:
                     copy.start()
             elif j + 3 < blocks + ahead:
-                stream(j + 3 - blocks).start()
+                stream(j + 3 - blocks)
             sums = lax.fori_loop(j * span // size, (j + 1) * span // size, gather, sums)
         r0, i0, r1, i1 = [jnp.sum(v, axis=0, keepdims=True) for v in sums]
         gr = jnp.sum(g_ref[:8, :], axis=0, keepdims=True)
@@ -310,7 +314,7 @@
 
                 @pl.when(m == later - ahead)
                 def _(later=later):
-                    stream(later).start()
+                    stream(later)
 
             acc = dot(a_ref[rows, :SLOTS], z_ref[0]) + dot(a_ref[rows, SLOTS:], z_ref[1])
             o_ref[m, :256, :] = acc.astype(BF)
@@ -341,13 +345,13 @@
 
 
 def finish(moved):
-    step = 64
+    step = 128
 
     def body(a_ref, e_ref, o_ref, c_ref):
-        for p in range(8):
-            for part in range(2):
-                lanes = pl.ds(part * 128, 128)
-                o_ref[pl.ds(2 * p + part, step, stride=16), :] = a_ref[p, :, lanes].astype(F32)
+        for part in range(2):
+            turned = jnp.swapaxes(a_ref[:, :, part * 128 : (part + 1) * 128].astype(F32), 0, 1)
+            for k in range(step):
+                o_ref[pl.ds(16 * k + part, 8, stride=2), :] = turned[k]
 
         @pl.when(pl.program_id(0) == 0)
         def _():

time: 124 us -> 108 us (0.87)
  blocking collectives: 41.8 us -> 17.6 us
  waiting for transfers between devices: 0.01 us -> 6.46 us
  starting transfers between devices: 7.92 us -> 12.5 us
  Pallas kernels: 71.7 us -> 68.5 us
    all_to_all x1 -> x0, blocking collectives: 20.6 us -> none  [local(): lax.all_to_all(sent, 'freq', split_axis=0, concat_axis=0, tiled=True)]
    all_to_all x0 -> x1, starting transfers between devices: none -> 4.58 us  [local(): lax.all_to_all(sent, 'freq', split_axis=0, concat_axis=0, tiled=True)]
    all_to_all x1, waiting for transfers between devices: 0.01 us -> 4.14 us  [local(): moved = lax.all_to_all(both, TRACE, split_axis=0, concat_axis=0, tiled=True)]
    all_to_all x1, blocking collectives: 21.3 us -> 17.6 us  [local(): moved = lax.all_to_all(sent, EIGHT, split_axis=0, concat_axis=0, tiled=True)]
    all_to_all x0 -> x1, waiting for transfers between devices: none -> 2.32 us  [local(): lax.all_to_all(sent, 'freq', split_axis=0, concat_axis=0, tiled=True)]
    pallas_call x2, Pallas kernels: 32.2 us -> 30.4 us  [make_atoms(): pl.pallas_call(body, grid=(count // rows,), out_shape=jax.ShapeDtypeStruc...]
    pallas_call x1, Pallas kernels: 4.01 us -> 2.58 us  [finish(): pl.pallas_call(body, grid=(256 // step,), out_shape=(jax.ShapeDtypeStruct...]
  transfers between devices with their start and end apart: 1 -> 2, of which waited for: 0 -> 2; matrix products, arithmetic and copies ran while one was open for 0% -> 0% of each run, Pallas kernels for 33% -> 37%
where the time goes in v4:
time: 108 us; the launch traced here: 107 us
  Pallas kernels  68.5 us (63%)
  blocking collectives  17.6 us (16%)
  starting transfers between devices  12.5 us (12%)
  waiting for transfers between devices  6.46 us (6%)
  other arithmetic  1.5 us (1%)
    pallas_call x2, Pallas kernels, make_atoms(): pl.pallas_call(body, grid=(count // rows,), out_shape=jax.ShapeDtypeStruc...  30.4 us
    pallas_call x1, Pallas kernels, pursue(): pl.pallas_call(body, out_shape=jax.ShapeDtypeStruct((8, 272, 256), BF), i...  18.7 us
    all_to_all x1, blocking collectives, local(): moved = lax.all_to_all(sent, EIGHT, split_axis=0, concat_axis=0, tiled=True)  17.6 us
    pallas_call x1, Pallas kernels, chosen_tables(): pl.pallas_call(body, grid=(SLOTS // size,), out_shape=(jax.ShapeDtypeStru...  9 us
    all_to_all x1, starting transfers between devices, local(): moved = lax.all_to_all(both, TRACE, split_axis=0, concat_axis=0, tiled=True)  7.92 us
    pallas_call x1, Pallas kernels, dft(): pl.pallas_call(body, grid=(1024 // width,), out_shape=jax.ShapeDtypeStruc...  7.83 us
    all_to_all x1, starting transfers between devices, local(): lax.all_to_all(sent, 'freq', split_axis=0, concat_axis=0, tiled=True)  4.58 us
    all_to_all x1, waiting for transfers between devices, local(): moved = lax.all_to_all(both, TRACE, split_axis=0, concat_axis=0, tiled=True)  4.14 us
  transfers between devices with their start and end apart: 2, of which 2 were waited for; matrix products, arithmetic and copies ran while one was open for 0% of the time, Pallas kernels for 37%

profile of v4, /device:TPU:0, one launch (start us, length us, event | category | flops | bytes accessed | tf_op | source)
XLA Modules:
  0.0 107.2 jit_solution(10840830256935590654)
XLA Ops:
  0.6 7.8 %dft.1 = bf16[8,256,256]{2,1,0:T(8,128)(2,1)} custom-call(bf16[256,4096]{1,0:T(8,128)(2,1)} %bitcast.4), custom_call_target="tpu_custom_call" | custom-call | flops 4294967296 | bytes 3145728 | tf_op jit(solution)/shard_map/dft/pallas_call | solution.py:103
  8.5 4.6 %all-to-all-start = ((bf16[8,256,256]{2,1,0:T(8,128)(2,1)}), bf16[8,256,256]{2,1,0:T(8,128)(2,1)S(1)}, u32[]{:S(2)}, u32[]{:S(2)}) async-start(bf16[8,256,256]{2,1,0:T(8,128)(2,1)} %dft.1), calls=%async_computation | async-start | bytes 2097152 | tf_op jit(solution)/shard_map/all_to_all | solution.py:386
  13.0 13.6 %atoms.2.rest_0_ = bf16[896,8192]{1,0:T(8,128)(2,1)} custom-call(s32[4,8,4096]{2,1,0:T(8,128)} %w_ref.5, s32[4,8,4096]{2,1,0:T(8,128)} %x_ref.5), custom_call_target="tpu_custom_call" | custom-call | flops 14092861440 | bytes 14680064 | tf_op jit(solution)/shard_map/atoms/pallas_call | solution.py:135
  26.6 2.3 %all-to-all-done = bf16[8,256,256]{2,1,0:T(8,128)(2,1)S(1)} async-done(((bf16[8,256,256]{2,1,0:T(8,128)(2,1)}), bf16[8,256,256]{2,1,0:T(8,128)(2,1)S(1)}, u32[]{:S(2)}, u32[]{:S(2)}) %all-to-all-start) | async-done | bytes 1048608 | tf_op jit(solution)/shard_map/all_to_all | solution.py:386
  29.0 1.5 %pad_maximum_fusion = bf16[16,256,256]{2,1,0:T(8,128)(2,1)} fusion(bf16[8,256,256]{2,1,0:T(8,128)(2,1)S(1)} %all-to-all-done), kind=kLoop, calls=%fused_computation | loop fusion | flops 1048576 | bytes 3145728 | tf_op jit(solution)/shard_map/concatenate | solution.py:387
  30.5 7.9 %all-to-all-start.1 = ((bf16[16,256,256]{2,1,0:T(8,128)(2,1)}), bf16[16,256,256]{2,1,0:T(8,128)(2,1)}, u32[]{:S(2)}, u32[]{:S(2)}) async-start(bf16[16,256,256]{2,1,0:T(8,128)(2,1)} %pad_maximum_fusion), calls=%async_computation.1 | async-start | bytes 4194304 | tf_op jit(solution)/shard_map/all_to_all | solution.py:388
  38.4 9.0 %tables.1 = (f32[4096,256]{1,0:T(8,128)}, f32[4096,256]{1,0:T(8,128)}, f32[16,128]{1,0:T(8,128)}) custom-call(s32[8]{0:T(128)} %fold_ref.3, s32[4,8,4096]{2,1,0:T(8,128)} %x_ref.5, s32[4,8,4096]{2,1,0:T(8,128)} %w_ref.5, s32[2,8,128]{2,1,0:T(8,128)} %ch_ref.1), custom_call_target="tpu_custom_call" | custom-call | flops 4294967296 | bytes 9437184 | tf_op jit(solution)/shard_map/tables/pallas_call | solution.py:188
  47.4 16.8 %atoms.3.rest_1_ = bf16[1152,8192]{1,0:T(8,128)(2,1)} custom-call(s32[4,8,4096]{2,1,0:T(8,128)} %w_ref.5, s32[4,8,4096]{2,1,0:T(8,128)} %x_ref.5), custom_call_target="tpu_custom_call" | custom-call | flops 18119393280 | bytes 18874368 | tf_op jit(solution)/shard_map/atoms/pallas_call | solution.py:135
  64.2 4.1 %all-to-all-done.1 = bf16[16,256,256]{2,1,0:T(8,128)(2,1)} async-done(((bf16[16,256,256]{2,1,0:T(8,128)(2,1)}), bf16[16,256,256]{2,1,0:T(8,128)(2,1)}, u32[]{:S(2)}, u32[]{:S(2)}) %all-to-all-start.1) | async-done | bytes 2097184 | tf_op jit(solution)/shard_map/all_to_all | solution.py:388
  68.3 18.7 %pursue.1 = bf16[8,272,256]{2,1,0:T(8,128)(2,1)} custom-call(s32[8]{0:T(128)} %fold_ref.3, f32[16,128]{1,0:T(8,128)} %get-tuple-element.7.g_ref, bf16[4096,256]{1,0:T(8,128)(2,1)} %bitcast.1.r_hbm, f32[4096,256]{1,0:T(8,128)} %get-tuple-element.8.c_hbm, f32[4096,256]{1,0:T(8,128)} %get-tuple-element.9.s_hbm, bf16[896,8192]{1,0:T(8,128)(2,1)} %atoms.2.rest_0_, ...), custom_call_target="tpu_custom_call" | custom-call | flops 9663676416 | bytes 47185920 | tf_op jit(solution)/shard_map/pursue/pallas_call | solution.py:327
  87.0 17.6 %all_to_all.15.a_ref.e_ref = bf16[8,272,256]{2,1,0:T(8,128)(2,1)} all-to-all(bf16[8,272,256]{2,1,0:T(8,128)(2,1)} %pursue.1), channel_id=1, replica_groups=mesh['freq'=8,'half'=2,'xl'=2,'z'=4] {'xl','z'}, dimensions={0} | all-to-all | bytes 2228224 | tf_op jit(solution)/shard_map/all_to_all | solution.py:393
  104.6 2.6 %finish.1 = (f32[4096,128]{1,0:T(8,128)}, f32[32,128]{1,0:T(8,128)}) custom-call(bf16[8,272,256]{2,1,0:T(8,128)(2,1)} %all_to_all.15.a_ref.e_ref, bf16[8,272,256]{2,1,0:T(8,128)(2,1)} %all_to_all.15.a_ref.e_ref), custom_call_target="tpu_custom_call" | custom-call | flops 1048576 | bytes 3145728 | tf_op jit(solution)/shard_map/finish/pallas_call | solution.py:366
Async XLA Ops:
  8.5 20.5 %all-to-all-start = ((bf16[8,256,256]{2,1,0:T(8,128)(2,1)}), bf16[8,256,256]{2,1,0:T(8,128)(2,1)S(1)}, u32[]{:S(2)}, u32[]{:S(2)}) async-start(bf16[8,256,256]{2,1,0:T(8,128)(2,1)} %dft.1), calls=%async_computation | async-start | bytes 2097152 | tf_op jit(solution)/shard_map/all_to_all | solution.py:386
  30.5 37.8 %all-to-all-start.1 = ((bf16[16,256,256]{2,1,0:T(8,128)(2,1)}), bf16[16,256,256]{2,1,0:T(8,128)(2,1)}, u32[]{:S(2)}, u32[]{:S(2)}) async-start(bf16[16,256,256]{2,1,0:T(8,128)(2,1)} %pad_maximum_fusion), calls=%async_computation.1 | async-start | bytes 4194304 | tf_op jit(solution)/shard_map/all_to_all | solution.py:388

commit v5 on v4

--- a/solution.py
+++ b/solution.py
@@ -285,7 +285,7 @@
 
         packed = [jnp.concatenate(pair, axis=1) for pair in zip(split(a0), split(b0))]
         packed += [jnp.concatenate(pair, axis=1) for pair in zip(split(a1), split(b1))]
-        packed = jnp.concatenate(packed + [jnp.zeros((10, 256), F32)], axis=0).astype(BF)
+        packed = jnp.concatenate(packed + [jnp.zeros((2, 256), F32)], axis=0).astype(BF)
         for b in range(8):
             o_ref[b, 256:, :] = packed
 
@@ -326,7 +326,7 @@
     whole = pl.BlockSpec(memory_space=pltpu.VMEM)
     return pl.pallas_call(
         body,
-        out_shape=jax.ShapeDtypeStruct((8, 272, 256), BF),
+        out_shape=jax.ShapeDtypeStruct((8, 264, 256), BF),
         in_specs=[pl.BlockSpec(memory_space=pltpu.SMEM), whole] + [hbm] * (3 + parts),
         out_specs=whole,
         scratch_shapes=[
@@ -338,7 +338,7 @@
             pltpu.SemaphoreType.DMA((blocks, 3)),
             pltpu.SemaphoreType.DMA((2048 // tall,)),
         ],
-        compiler_params=pltpu.CompilerParams(vmem_limit_bytes=VMEM),
+        compiler_params=pltpu.CompilerParams(vmem_limit_bytes=50 << 20),
         cost_estimate=pl.CostEstimate(flops=9 << 30, bytes_accessed=45 << 20, transcendentals=0),
         name="pursue",
     )(fold, cross, received, cosine, sine, *atoms)
@@ -369,13 +369,13 @@
         out_shape=(jax.ShapeDtypeStruct((4096, 128), F32), jax.ShapeDtypeStruct((32, 128), F32)),
         in_specs=[
             pl.BlockSpec((8, step, 256), lambda i: (0, i, 0)),
-            pl.BlockSpec((8, 16, 256), lambda i: (0, 16, 0)),
+            pl.BlockSpec((8, 8, 256), lambda i: (0, 32, 0)),
         ],
         out_specs=(
             pl.BlockSpec((step * 16, 128), lambda i: (i, 0)),
             pl.BlockSpec((32, 128), lambda i: (0, 0)),
         ),
-        compiler_params=pltpu.CompilerParams(vmem_limit_bytes=VMEM),
+        compiler_params=pltpu.CompilerParams(vmem_limit_bytes=16 << 20),
         cost_estimate=pl.CostEstimate(flops=1 << 20, bytes_accessed=3 << 20, transcendentals=0),
         name="finish",
     )(moved, moved)

time: 108 us -> 105 us (0.972)
  Pallas kernels: 68.5 us -> 66.4 us
    pallas_call x1, Pallas kernels: 18.7 us -> 17.5 us  [pursue(): pl.pallas_call(body, out_shape=jax.ShapeDtypeStruct((8, 264, 256), BF), i...]
  transfers between devices with their start and end apart: 2 -> 2, of which waited for: 2 -> 2; matrix products, arithmetic and copies ran while one was open for 0% -> 0% of each run, Pallas kernels for 37% -> 38%
where the time goes in v5:
time: 105 us
  Pallas kernels  66.4 us (63%)
  blocking collectives  17 us (16%)
  starting transfers between devices  12.5 us (12%)
  waiting for transfers between devices  6.43 us (6%)
  other arithmetic  1.5 us (1%)
    pallas_call x2, Pallas kernels, make_atoms(): pl.pallas_call(body, grid=(count // rows,), out_shape=jax.ShapeDtypeStruc...  30.4 us
    pallas_call x1, Pallas kernels, pursue(): pl.pallas_call(body, out_shape=jax.ShapeDtypeStruct((8, 264, 256), BF), i...  17.5 us
    all_to_all x1, blocking collectives, local(): moved = lax.all_to_all(sent, EIGHT, split_axis=0, concat_axis=0, tiled=True)  17 us
    pallas_call x1, Pallas kernels, chosen_tables(): pl.pallas_call(body, grid=(SLOTS // size,), out_shape=(jax.ShapeDtypeStru...  9 us
    all_to_all x1, starting transfers between devices, local(): moved = lax.all_to_all(both, TRACE, split_axis=0, concat_axis=0, tiled=True)  7.92 us
    pallas_call x1, Pallas kernels, dft(): pl.pallas_call(body, grid=(1024 // width,), out_shape=jax.ShapeDtypeStruc...  7.83 us
    all_to_all x1, starting transfers between devices, local(): lax.all_to_all(sent, 'freq', split_axis=0, concat_axis=0, tiled=True)  4.58 us
    all_to_all x1, waiting for transfers between devices, local(): moved = lax.all_to_all(both, TRACE, split_axis=0, concat_axis=0, tiled=True)  4.1 us
  transfers between devices with their start and end apart: 2, of which 2 were waited for; matrix products, arithmetic and copies ran while one was open for 0% of the time, Pallas kernels for 38%

profile of v5, /device:TPU:0, one launch (start us, length us, event | category | flops | bytes accessed | tf_op | source)
XLA Modules:
  0.0 104.5 jit_solution(7122451758872896823)
XLA Ops:
  0.6 7.8 %dft.1 = bf16[8,256,256]{2,1,0:T(8,128)(2,1)} custom-call(bf16[256,4096]{1,0:T(8,128)(2,1)} %bitcast.4), custom_call_target="tpu_custom_call" | custom-call | flops 4294967296 | bytes 3145728 | tf_op jit(solution)/shard_map/dft/pallas_call | solution.py:103
  8.5 4.6 %all-to-all-start = ((bf16[8,256,256]{2,1,0:T(8,128)(2,1)}), bf16[8,256,256]{2,1,0:T(8,128)(2,1)S(1)}, u32[]{:S(2)}, u32[]{:S(2)}) async-start(bf16[8,256,256]{2,1,0:T(8,128)(2,1)} %dft.1), calls=%async_computation | async-start | bytes 2097152 | tf_op jit(solution)/shard_map/all_to_all | solution.py:386
  13.0 13.6 %atoms.2.rest_0_ = bf16[896,8192]{1,0:T(8,128)(2,1)} custom-call(s32[4,8,4096]{2,1,0:T(8,128)} %w_ref.5, s32[4,8,4096]{2,1,0:T(8,128)} %x_ref.5), custom_call_target="tpu_custom_call" | custom-call | flops 14092861440 | bytes 14680064 | tf_op jit(solution)/shard_map/atoms/pallas_call | solution.py:135
  26.6 2.3 %all-to-all-done = bf16[8,256,256]{2,1,0:T(8,128)(2,1)S(1)} async-done(((bf16[8,256,256]{2,1,0:T(8,128)(2,1)}), bf16[8,256,256]{2,1,0:T(8,128)(2,1)S(1)}, u32[]{:S(2)}, u32[]{:S(2)}) %all-to-all-start) | async-done | bytes 1048608 | tf_op jit(solution)/shard_map/all_to_all | solution.py:386
  29.0 1.5 %pad_maximum_fusion = bf16[16,256,256]{2,1,0:T(8,128)(2,1)} fusion(bf16[8,256,256]{2,1,0:T(8,128)(2,1)S(1)} %all-to-all-done), kind=kLoop, calls=%fused_computation | loop fusion | flops 1048576 | bytes 3145728 | tf_op jit(solution)/shard_map/concatenate | solution.py:387
  30.5 7.9 %all-to-all-start.1 = ((bf16[16,256,256]{2,1,0:T(8,128)(2,1)}), bf16[16,256,256]{2,1,0:T(8,128)(2,1)}, u32[]{:S(2)}, u32[]{:S(2)}) async-start(bf16[16,256,256]{2,1,0:T(8,128)(2,1)} %pad_maximum_fusion), calls=%async_computation.1 | async-start | bytes 4194304 | tf_op jit(solution)/shard_map/all_to_all | solution.py:388
  38.4 9.0 %tables.1 = (f32[4096,256]{1,0:T(8,128)}, f32[4096,256]{1,0:T(8,128)}, f32[16,128]{1,0:T(8,128)}) custom-call(s32[8]{0:T(128)} %fold_ref.3, s32[4,8,4096]{2,1,0:T(8,128)} %x_ref.5, s32[4,8,4096]{2,1,0:T(8,128)} %w_ref.5, s32[2,8,128]{2,1,0:T(8,128)} %ch_ref.1), custom_call_target="tpu_custom_call" | custom-call | flops 4294967296 | bytes 9437184 | tf_op jit(solution)/shard_map/tables/pallas_call | solution.py:188
  47.4 0.0 copy-start
  47.4 0.0 copy-start.1
  47.4 16.8 %atoms.3.rest_1_ = bf16[1152,8192]{1,0:T(8,128)(2,1)} custom-call(s32[4,8,4096]{2,1,0:T(8,128)} %w_ref.5, s32[4,8,4096]{2,1,0:T(8,128)} %x_ref.5), custom_call_target="tpu_custom_call" | custom-call | flops 18119393280 | bytes 18874368 | tf_op jit(solution)/shard_map/atoms/pallas_call | solution.py:135
  64.2 4.1 %all-to-all-done.1 = bf16[16,256,256]{2,1,0:T(8,128)(2,1)} async-done(((bf16[16,256,256]{2,1,0:T(8,128)(2,1)}), bf16[16,256,256]{2,1,0:T(8,128)(2,1)}, u32[]{:S(2)}, u32[]{:S(2)}) %all-to-all-start.1) | async-done | bytes 2097184 | tf_op jit(solution)/shard_map/all_to_all | solution.py:388
  68.3 0.0 copy-done
  68.3 0.0 copy-done.1
  68.3 17.5 %pursue.1 = bf16[8,264,256]{2,1,0:T(8,128)(2,1)S(1)} custom-call(s32[8]{0:T(128)S(1)} %copy-done.1, f32[16,128]{1,0:T(8,128)S(1)} %copy-done, bf16[4096,256]{1,0:T(8,128)(2,1)} %bitcast.1.r_hbm, f32[4096,256]{1,0:T(8,128)} %get-tuple-element.8.c_hbm, f32[4096,256]{1,0:T(8,128)} %get-tuple-element.9.s_hbm, bf16[896,8192]{1,0:T(8,128)(2,1)} %atoms.2.rest_0_, ...), custom_call_target="tpu_custom_call" | custom-call | flops 9663676416 | bytes 47185920 | tf_op jit(solution)/shard_map/pursue/pallas_call | solution.py:327
  85.9 17.0 %all_to_all.15.a_ref.e_ref = bf16[8,264,256]{2,1,0:T(8,128)(2,1)S(1)} all-to-all(bf16[8,264,256]{2,1,0:T(8,128)(2,1)S(1)} %pursue.1), channel_id=1, replica_groups=mesh['freq'=8,'half'=2,'xl'=2,'z'=4] {'xl','z'}, dimensions={0} | all-to-all | bytes 2162688 | tf_op jit(solution)/shard_map/all_to_all | solution.py:393
  102.9 1.6 %finish.1 = (f32[4096,128]{1,0:T(8,128)}, f32[32,128]{1,0:T(8,128)}) custom-call(bf16[8,264,256]{2,1,0:T(8,128)(2,1)S(1)} %all_to_all.15.a_ref.e_ref, bf16[8,264,256]{2,1,0:T(8,128)(2,1)S(1)} %all_to_all.15.a_ref.e_ref), custom_call_target="tpu_custom_call" | custom-call | flops 1048576 | bytes 3145728 | tf_op jit(solution)/shard_map/finish/pallas_call | solution.py:366
Async XLA Ops:
  8.5 20.5 %all-to-all-start = ((bf16[8,256,256]{2,1,0:T(8,128)(2,1)}), bf16[8,256,256]{2,1,0:T(8,128)(2,1)S(1)}, u32[]{:S(2)}, u32[]{:S(2)}) async-start(bf16[8,256,256]{2,1,0:T(8,128)(2,1)} %dft.1), calls=%async_computation | async-start | bytes 2097152 | tf_op jit(solution)/shard_map/all_to_all | solution.py:386
  30.5 37.8 %all-to-all-start.1 = ((bf16[16,256,256]{2,1,0:T(8,128)(2,1)}), bf16[16,256,256]{2,1,0:T(8,128)(2,1)}, u32[]{:S(2)}, u32[]{:S(2)}) async-start(bf16[16,256,256]{2,1,0:T(8,128)(2,1)} %pad_maximum_fusion), calls=%async_computation.1 | async-start | bytes 4194304 | tf_op jit(solution)/shard_map/all_to_all | solution.py:388
  47.4 20.9 %copy-start = (f32[16,128]{1,0:T(8,128)S(1)}, f32[16,128]{1,0:T(8,128)}, u32[]{:S(2)}) copy-start(f32[16,128]{1,0:T(8,128)} %get-tuple-element.7.g_ref) | copy-start | bytes 24580
  47.4 20.9 %copy-start.1 = (s32[8]{0:T(128)S(1)}, s32[8]{0:T(128)}, u32[]{:S(2)}) copy-start(s32[8]{0:T(128)} %fold_ref.3) | copy-start | bytes 100

commit v6 on v5

--- a/solution.py
+++ b/solution.py
@@ -112,6 +112,26 @@
     )(traces)
 
 
+def twice(blocks):
+    def body(x_ref, o_ref, sem):
+        copies = [pltpu.make_async_copy(x_ref, o_ref.at[pl.ds(8 * k, 8)], sem.at[k]) for k in range(2)]
+        for copy in copies:
+            copy.start()
+        for copy in copies:
+            copy.wait()
+
+    return pl.pallas_call(
+        body,
+        out_shape=jax.ShapeDtypeStruct((16, 256, 256), BF),
+        in_specs=[pl.BlockSpec(memory_space=pltpu.VMEM)],
+        out_specs=pl.BlockSpec(memory_space=pl.ANY),
+        scratch_shapes=[pltpu.SemaphoreType.DMA((2,))],
+        compiler_params=pltpu.CompilerParams(vmem_limit_bytes=8 << 20),
+        cost_estimate=pl.CostEstimate(flops=1 << 20, bytes_accessed=3 << 20, transcendentals=0),
+        name="twice",
+    )(blocks)
+
+
 def make_atoms(waves, places, first, count):
     rows = 128
 
@@ -191,7 +211,7 @@
         out_shape=(
             jax.ShapeDtypeStruct((SLOTS, 256), F32),
             jax.ShapeDtypeStruct((SLOTS, 256), F32),
-            jax.ShapeDtypeStruct((16, 128), F32),
+            jax.ShapeDtypeStruct((16, 1 << 17), F32),
         ),
         in_specs=[
             pl.BlockSpec(memory_space=pltpu.SMEM),
@@ -216,9 +236,11 @@
     span = SLOTS // blocks
     parts = len(atoms)
 
-    def body(fold_ref, g_ref, r_hbm, c_hbm, s_hbm, *rest):
-        a_hbm, (o_ref, r_ref, c_ref, s_ref, a_ref, z_ref, sem, a_sem) = rest[:parts], rest[parts:]
+    def body(fold_ref, g_hbm, r_hbm, c_hbm, s_hbm, *rest):
+        a_hbm, (o_ref, g_ref, r_ref, c_ref, s_ref, a_ref, z_ref, g_sem, sem, a_sem) = rest[:parts], rest[parts:]
         patch = lax.axis_index("xl") * 4 + lax.axis_index("z")
+        cross_copy = pltpu.make_async_copy(g_hbm.at[:, :128], g_ref, g_sem)
+        cross_copy.start()
         loads = []
         for j in range(blocks):
             rows = pl.ds(j * span, span)
@@ -272,6 +294,7 @@
                 stream(j + 3 - blocks)
             sums = lax.fori_loop(j * span // size, (j + 1) * span // size, gather, sums)
         r0, i0, r1, i1 = [jnp.sum(v, axis=0, keepdims=True) for v in sums]
+        cross_copy.wait()
         gr = jnp.sum(g_ref[:8, :], axis=0, keepdims=True)
         gi = jnp.sum(g_ref[8:, :], axis=0, keepdims=True)
         a0, b0 = r0 * inverse, i0 * inverse
@@ -327,18 +350,20 @@
     return pl.pallas_call(
         body,
         out_shape=jax.ShapeDtypeStruct((8, 264, 256), BF),
-        in_specs=[pl.BlockSpec(memory_space=pltpu.SMEM), whole] + [hbm] * (3 + parts),
+        in_specs=[pl.BlockSpec(memory_space=pltpu.SMEM)] + [hbm] * (4 + parts),
         out_specs=whole,
         scratch_shapes=[
+            pltpu.VMEM((16, 128), F32),
             pltpu.VMEM((SLOTS, 256), BF),
             pltpu.VMEM((SLOTS, 256), F32),
             pltpu.VMEM((SLOTS, 256), F32),
             pltpu.VMEM((2048, 2 * SLOTS), BF),
             pltpu.VMEM((2, SLOTS, 256), BF),
+            pltpu.SemaphoreType.DMA(()),
             pltpu.SemaphoreType.DMA((blocks, 3)),
             pltpu.SemaphoreType.DMA((2048 // tall,)),
         ],
-        compiler_params=pltpu.CompilerParams(vmem_limit_bytes=50 << 20),
+        compiler_params=pltpu.CompilerParams(vmem_limit_bytes=52 << 20),
         cost_estimate=pl.CostEstimate(flops=9 << 30, bytes_accessed=45 << 20, transcendentals=0),
         name="pursue",
     )(fold, cross, received, cosine, sine, *atoms)
@@ -384,7 +409,7 @@
 def local(traces, coords, wavenumbers, fold, selected):
     sent = dft(traces[0])
     moved = lax.all_to_all(sent, "freq", split_axis=0, concat_axis=0, tiled=True)
-    both = jnp.concatenate([moved, moved], axis=0)
+    both = twice(moved)
     moved = lax.all_to_all(both, TRACE, split_axis=0, concat_axis=0, tiled=True)
     early = make_atoms(wavenumbers, coords, 0, EARLY)
     late = make_atoms(wavenumbers, coords, EARLY, 2048 - EARLY)

time: 105 us -> 106 us (level)
  Pallas kernels: 66.4 us -> 68.7 us
  other arithmetic: 1.5 us -> 0 us
    concatenate x1 -> x0, other arithmetic: 1.5 us -> none  [local(): both = jnp.concatenate([moved, moved], axis=0)]
    pallas_call x0 -> x1, Pallas kernels: none -> 1.33 us  [twice(): pl.pallas_call(body, out_shape=jax.ShapeDtypeStruct((16, 256, 256), BF),...]
  transfers between devices with their start and end apart: 2 -> 2, of which waited for: 2 -> 2; matrix products, arithmetic and copies ran while one was open for 0% -> 0% of each run, Pallas kernels for 38% -> 37%
where the time goes in v6:
time: 106 us; the launch traced here: 105 us
  Pallas kernels  68.7 us (65%)
  blocking collectives  17 us (16%)
  starting transfers between devices  12.5 us (12%)
  waiting for transfers between devices  6.39 us (6%)
    pallas_call x2, Pallas kernels, make_atoms(): pl.pallas_call(body, grid=(count // rows,), out_shape=jax.ShapeDtypeStruc...  30.4 us
    pallas_call x1, Pallas kernels, pursue(): pl.pallas_call(body, out_shape=jax.ShapeDtypeStruct((8, 264, 256), BF), i...  18.5 us
    all_to_all x1, blocking collectives, local(): moved = lax.all_to_all(sent, EIGHT, split_axis=0, concat_axis=0, tiled=True)  17 us
    pallas_call x1, Pallas kernels, chosen_tables(): pl.pallas_call(body, grid=(SLOTS // size,), out_shape=(jax.ShapeDtypeStru...  9.04 us
    all_to_all x1, starting transfers between devices, local(): moved = lax.all_to_all(both, TRACE, split_axis=0, concat_axis=0, tiled=True)  7.94 us
    pallas_call x1, Pallas kernels, dft(): pl.pallas_call(body, grid=(1024 // width,), out_shape=jax.ShapeDtypeStruc...  7.83 us
    all_to_all x1, starting transfers between devices, local(): lax.all_to_all(sent, 'freq', split_axis=0, concat_axis=0, tiled=True)  4.58 us
    all_to_all x1, waiting for transfers between devices, local(): moved = lax.all_to_all(both, TRACE, split_axis=0, concat_axis=0, tiled=True)  4.07 us
  transfers between devices with their start and end apart: 2, of which 2 were waited for; matrix products, arithmetic and copies ran while one was open for 0% of the time, Pallas kernels for 37%

profile of v6, /device:TPU:0, one launch (start us, length us, event | category | flops | bytes accessed | tf_op | source)
XLA Modules:
  0.0 105.3 jit_solution(9884458027464642384)
XLA Ops:
  0.6 7.8 %dft.1 = bf16[8,256,256]{2,1,0:T(8,128)(2,1)} custom-call(bf16[256,4096]{1,0:T(8,128)(2,1)} %bitcast.4), custom_call_target="tpu_custom_call" | custom-call | flops 4294967296 | bytes 3145728 | tf_op jit(solution)/shard_map/dft/pallas_call | solution.py:103
  8.5 4.6 %all-to-all-start = ((bf16[8,256,256]{2,1,0:T(8,128)(2,1)}), bf16[8,256,256]{2,1,0:T(8,128)(2,1)S(1)}, u32[]{:S(2)}, u32[]{:S(2)}) async-start(bf16[8,256,256]{2,1,0:T(8,128)(2,1)} %dft.1), calls=%async_computation | async-start | bytes 2097152 | tf_op jit(solution)/shard_map/all_to_all | solution.py:411
  13.0 13.6 %atoms.2.rest_0_ = bf16[896,8192]{1,0:T(8,128)(2,1)} custom-call(s32[4,8,4096]{2,1,0:T(8,128)} %w_ref.5, s32[4,8,4096]{2,1,0:T(8,128)} %x_ref.5), custom_call_target="tpu_custom_call" | custom-call | flops 14092861440 | bytes 14680064 | tf_op jit(solution)/shard_map/atoms/pallas_call | solution.py:155
  26.6 2.3 %all-to-all-done.x_ref = bf16[8,256,256]{2,1,0:T(8,128)(2,1)S(1)} async-done(((bf16[8,256,256]{2,1,0:T(8,128)(2,1)}), bf16[8,256,256]{2,1,0:T(8,128)(2,1)S(1)}, u32[]{:S(2)}, u32[]{:S(2)}) %all-to-all-start) | async-done | bytes 1048608 | tf_op jit(solution)/shard_map/all_to_all | solution.py:411
  29.0 1.3 %twice.1 = bf16[16,256,256]{2,1,0:T(8,128)(2,1)} custom-call(bf16[8,256,256]{2,1,0:T(8,128)(2,1)S(1)} %all-to-all-done.x_ref), custom_call_target="tpu_custom_call" | custom-call | flops 1048576 | bytes 3145728 | tf_op jit(solution)/shard_map/twice/pallas_call | solution.py:123
  30.3 7.9 %all-to-all-start.1 = ((bf16[16,256,256]{2,1,0:T(8,128)(2,1)}), bf16[16,256,256]{2,1,0:T(8,128)(2,1)}, u32[]{:S(2)}, u32[]{:S(2)}) async-start(bf16[16,256,256]{2,1,0:T(8,128)(2,1)} %twice.1), calls=%async_computation.1 | async-start | bytes 4194304 | tf_op jit(solution)/shard_map/all_to_all | solution.py:413
  38.3 9.0 %tables.1 = (f32[4096,256]{1,0:T(8,128)}, f32[4096,256]{1,0:T(8,128)}, f32[16,131072]{1,0:T(8,128)}) custom-call(s32[8]{0:T(128)} %fold_ref.3, s32[4,8,4096]{2,1,0:T(8,128)} %x_ref.5, s32[4,8,4096]{2,1,0:T(8,128)} %w_ref.5, s32[2,8,128]{2,1,0:T(8,128)} %ch_ref.1), custom_call_target="tpu_custom_call" | custom-call | flops 4294967296 | bytes 9437184 | tf_op jit(solution)/shard_map/tables/pallas_call | solution.py:208
  47.3 0.0 copy-start
  47.3 16.8 %atoms.3.rest_1_ = bf16[1152,8192]{1,0:T(8,128)(2,1)} custom-call(s32[4,8,4096]{2,1,0:T(8,128)} %w_ref.5, s32[4,8,4096]{2,1,0:T(8,128)} %x_ref.5), custom_call_target="tpu_custom_call" | custom-call | flops 18119393280 | bytes 18874368 | tf_op jit(solution)/shard_map/atoms/pallas_call | solution.py:155
  64.1 4.1 %all-to-all-done.1 = bf16[16,256,256]{2,1,0:T(8,128)(2,1)} async-done(((bf16[16,256,256]{2,1,0:T(8,128)(2,1)}), bf16[16,256,256]{2,1,0:T(8,128)(2,1)}, u32[]{:S(2)}, u32[]{:S(2)}) %all-to-all-start.1) | async-done | bytes 2097184 | tf_op jit(solution)/shard_map/all_to_all | solution.py:413
  68.2 0.0 copy-done
  68.2 18.5 %pursue.1 = bf16[8,264,256]{2,1,0:T(8,128)(2,1)S(1)} custom-call(s32[8]{0:T(128)S(1)} %copy-done, f32[16,131072]{1,0:T(8,128)} %get-tuple-element.7.g_hbm, bf16[4096,256]{1,0:T(8,128)(2,1)} %bitcast.1.r_hbm, f32[4096,256]{1,0:T(8,128)} %get-tuple-element.8.c_hbm, f32[4096,256]{1,0:T(8,128)} %get-tuple-element.9.s_hbm, bf16[896,8192]{1,0:T(8,128)(2,1)} %atoms.2.rest_0_, ...), custom_call_target="tpu_custom_call" | custom-call | flops 9663676416 | bytes 47185920 | tf_op jit(solution)/shard_map/pursue/pallas_call | solution.py:350
  86.6 17.0 %all_to_all.15.a_ref.e_ref = bf16[8,264,256]{2,1,0:T(8,128)(2,1)S(1)} all-to-all(bf16[8,264,256]{2,1,0:T(8,128)(2,1)S(1)} %pursue.1), channel_id=1, replica_groups=mesh['freq'=8,'half'=2,'xl'=2,'z'=4] {'xl','z'}, dimensions={0} | all-to-all | bytes 2162688 | tf_op jit(solution)/shard_map/all_to_all | solution.py:418
  103.6 1.6 %finish.1 = (f32[4096,128]{1,0:T(8,128)}, f32[32,128]{1,0:T(8,128)}) custom-call(bf16[8,264,256]{2,1,0:T(8,128)(2,1)S(1)} %all_to_all.15.a_ref.e_ref, bf16[8,264,256]{2,1,0:T(8,128)(2,1)S(1)} %all_to_all.15.a_ref.e_ref), custom_call_target="tpu_custom_call" | custom-call | flops 1048576 | bytes 3145728 | tf_op jit(solution)/shard_map/finish/pallas_call | solution.py:391
Async XLA Ops:
  8.5 20.5 %all-to-all-start = ((bf16[8,256,256]{2,1,0:T(8,128)(2,1)}), bf16[8,256,256]{2,1,0:T(8,128)(2,1)S(1)}, u32[]{:S(2)}, u32[]{:S(2)}) async-start(bf16[8,256,256]{2,1,0:T(8,128)(2,1)} %dft.1), calls=%async_computation | async-start | bytes 2097152 | tf_op jit(solution)/shard_map/all_to_all | solution.py:411
  30.3 37.8 %all-to-all-start.1 = ((bf16[16,256,256]{2,1,0:T(8,128)(2,1)}), bf16[16,256,256]{2,1,0:T(8,128)(2,1)}, u32[]{:S(2)}, u32[]{:S(2)}) async-start(bf16[16,256,256]{2,1,0:T(8,128)(2,1)} %twice.1), calls=%async_computation.1 | async-start | bytes 4194304 | tf_op jit(solution)/shard_map/all_to_all | solution.py:413
  47.3 20.9 %copy-start = (s32[8]{0:T(128)S(1)}, s32[8]{0:T(128)}, u32[]{:S(2)}) copy-start(s32[8]{0:T(128)} %fold_ref.3) | copy-start | bytes 100
